TPU v7x, 256 devices: a whole 4x4x8 slice. The times are simulated.
256 devices in a mesh: period: 128 (over z, x, y), half: 2 (over core).
Axes of the slice: x: 4, y: 4, z: 8, core: 2. Of those that a mesh axis runs over, the one named last changes fastest.
Arguments:
- probes: float32 [1024, 4, 512], P('period', None, 'half'), may hold values from -6 to 6
- footprints: bfloat16 [1024, 512, 512], P('period', None, 'half'), may hold values from -0.25 to 0.25
- lag_weights: float32 [1024, 4], P('period'), may hold values from 0.2 to 2
- owners: int32 [1024, 4], P('period'), may hold values from 0 to 127, all different within a row; in each aligned block of 8 rows (0 to 7, 8 to 15, ...) at most 2 rows name the same one
- window_tiles: int32 [1024, 2], P('period', 'half'), may hold values from 0 to 10
- coords: int32 [2, 3072], replicated, may hold values from 0 to 63
- temporal: float32 [128, 128], replicated, as said below
Outputs:
- coefficients: float32 [4, 4], replicated
- residual: float32 [1024, 4, 512], P('period', None, 'half')
Inputs may be any that keep to these rules, and one draw needn't show every extreme that they name: `owners`: each row names 4 different periods. Among the 8 rows of one index of period, no period is named more than 2 times, and one is named exactly 2 times. `temporal`: symmetric.
All inputs are finite; a program needn't handle non-finite values.
Results may differ from a plain program's by a relative error of at most 0.025.
Values may be sent and summed in bfloat16 or wider, within the bound.
No kernel may reach another device: no remote copies, remote signals or barrier semaphores. Data moves between devices by JAX's collectives and lax.ppermute only.
A program may use at most 64 MiB of HBM per device.

v0:
```python
import functools

import jax
import jax.numpy as jnp
from jax import lax
from jax.experimental import pallas as pl
from jax.experimental.pallas import tpu as pltpu
from jax.sharding import PartitionSpec as P


epsilon = 1e-06
kernel_scale = 0.05
kernel_length = 6.0
log2e = 1.4426950408889634
LANES = 128
HALF_LANES = 64
HALF_SUBLANES = 4
GROUP = 48


smem = pl.BlockSpec(memory_space=pltpu.SMEM)
vmem = pl.BlockSpec(memory_space=pltpu.VMEM)
hbm = pl.BlockSpec(memory_space=pltpu.HBM)
small = pltpu.CompilerParams(vmem_limit_bytes=24 * 1024 * 1024)


def in_hbm(value):
    return pltpu.with_memory_space_constraint(value, pltpu.HBM)


def in_vmem(value):
    return pltpu.with_memory_space_constraint(value, pltpu.VMEM)


def from_other_half(value):
    return lax.ppermute(value, "half", [(0, 1), (1, 0)])


def exchange(value):
    return lax.all_to_all(value, "period", split_axis=0, concat_axis=0, tiled=True)


def block_of_row(shape, block_count):
    return lax.rem(lax.broadcasted_iota(jnp.int32, shape, 0), block_count)


def halves(value):
    high = value.astype(jnp.bfloat16)
    low = (value - high.astype(jnp.float32)).astype(jnp.bfloat16)
    return high, low


def dot(left, right, dims=((1,), (0,))):
    return lax.dot_general(left, right, (dims, ((), ())), preferred_element_type=jnp.float32)


def tile_iotas():
    row = lax.broadcasted_iota(jnp.int32, (2 * HALF_SUBLANES, LANES), 0)
    lane = lax.broadcasted_iota(jnp.int32, (2 * HALF_SUBLANES, LANES), 1)
    return row, lane


def half_turn(tile):
    return pltpu.roll(tile, HALF_SUBLANES, 0)


def swap_quarters(tile):
    row, lane = tile_iotas()
    turned = half_turn(pltpu.roll(tile, HALF_LANES, 1))
    return jnp.where((row < HALF_SUBLANES) == (lane < HALF_LANES), tile, turned)


def group_span(group):
    return divmod(GROUP * group, LANES)


def pack_groups(tiles):
    row, lane = tile_iotas()
    left = lane < HALF_LANES
    diagonal = (row < HALF_SUBLANES) == left
    packed = []
    for pair in range(4):
        first, second = [], []
        for group in (2 * pair, 2 * pair + 1):
            place, at = group_span(group)
            source = tiles[place]
            if at + GROUP > LANES:
                source = jnp.where(lane >= at, source, tiles[place + 1])
            for target, end in ((first, 0), (second, HALF_LANES)):
                shift = (end - at) % LANES
                target.append(pltpu.roll(source, shift, 1) if shift else source)
        kept = jnp.where(left, first[0], second[1])
        moved = half_turn(jnp.where(left, first[1], second[0]))
        packed.append(jnp.where(diagonal, kept, moved))
    return packed


def unpack_groups(packed):
    row, lane = tile_iotas()
    upper = row < HALF_SUBLANES
    groups = []
    for tile in packed:
        turned = pltpu.roll(tile, HALF_LANES, 1)
        groups.append(jnp.where(upper, tile, half_turn(turned)))
        groups.append(jnp.where(upper, half_turn(tile), turned))
    tiles = [None, None, None]
    for group, value in enumerate(groups):
        place, at = group_span(group)
        value = pltpu.roll(value, at, 1) if at else value
        tiles[place] = value if at == 0 else jnp.where(lane >= at, value, tiles[place])
        if at + GROUP > LANES:
            tiles[place + 1] = value
    return tiles


def adjoint_pieces(vector, feet_ref):
    block_count, _, window = feet_ref.shape
    block_index = block_of_row((vector.shape[0], window), block_count)
    pieces = jnp.zeros((vector.shape[0], window), jnp.float32)
    for block in range(block_count):
        pieces = jnp.where(block_index == block, dot(vector, feet_ref[block]), pieces)
    return pieces


def placed_tile(pieces, tile_rows, tile, probe, probe_count):
    count = pieces.shape[0] // probe_count
    rows = slice(probe * count, (probe + 1) * count)
    value = jnp.where(tile_rows == tile, pieces[rows, :LANES], 0.0)
    return jnp.where(tile_rows == tile - 1, pieces[rows, LANES:], value)


def distance_terms(cells, turned):
    x, y = cells[0:1], cells[1:2]
    norm = x * x + y * y
    low = (norm & 255).astype(jnp.float32)
    high = (norm - (norm & 255)).astype(jnp.float32)
    x, y, one = x.astype(jnp.float32), y.astype(jnp.float32), jnp.ones(x.shape, jnp.float32)
    if turned:
        terms = [-2.0 * x, -2.0 * y, one, one, high, low]
    else:
        terms = [x, y, high, low, one, one]
    row = lax.broadcasted_iota(jnp.int32, (16, x.shape[1]), 0)
    result = jnp.zeros((16, x.shape[1]), jnp.float32)
    for place, term in enumerate(terms):
        result = jnp.where(row == place, term, result)
    return result.astype(jnp.bfloat16)


def prepare_kernel(tiles_in, owners_in, weights_in, own_in, coords_in, feet_in, own_ref, table_ref, tile_rows_ref, left_ref, right_ref, feet_ref, tiles_ref, owners_ref, weights_ref, probes_ref, coords_ref, sems):
    block_count, probe_count, _ = probes_ref.shape
    top_count = owners_ref.shape[0]
    pairs = (
        (tiles_in, tiles_ref),
        (owners_in, owners_ref),
        (weights_in, weights_ref),
        (own_in, probes_ref),
        (coords_in, coords_ref),
        (feet_in, feet_ref),
    )
    copies = [
        pltpu.make_async_copy(source, target, sems.at[place])
        for place, (source, target) in enumerate(pairs)
    ]
    for copy in copies:
        copy.start()
    for copy in copies[:5]:
        copy.wait()
    for probe in range(probe_count):
        rows = slice(probe * block_count, (probe + 1) * block_count)
        own_ref[rows, :] = probes_ref[:, probe, :]
    row, lane = tile_iotas()
    owner = jnp.zeros(row.shape, jnp.float32)
    weight = jnp.zeros(row.shape, jnp.float32)
    for block in range(block_count):
        column, turn = divmod(block, HALF_SUBLANES)
        for top in range(top_count):
            here = lane == column * HALF_LANES + GROUP + top
            here = here & (lax.rem(row, HALF_SUBLANES) == turn)
            owner = jnp.where(here, owners_ref[top, block].astype(jnp.float32), owner)
            weight = jnp.where(here, weights_ref[top, block], weight)
    table = owner
    for part in range(1, 4):
        high = weight.astype(jnp.bfloat16).astype(jnp.float32)
        table = table + pltpu.roll(high, part * top_count, 1)
        weight = weight - high
    table_ref[...] = table
    tile_rows = jnp.zeros(row.shape, jnp.int32)
    for block in range(block_count):
        tile_rows = jnp.where(row == block, tiles_ref[block], tile_rows)
    tile_rows_ref[...] = tile_rows
    half = lax.axis_index("half")
    half_cells = left_ref.shape[1]
    own_at = pl.multiple_of(half * half_cells, LANES)
    other_at = pl.multiple_of((1 - half) * half_cells, LANES)
    own = coords_ref[:, pl.ds(own_at, half_cells)]
    left_ref[...] = distance_terms(own, False)
    right_ref[:, :half_cells] = distance_terms(own, True)
    right_ref[:, half_cells:] = distance_terms(coords_ref[:, pl.ds(other_at, half_cells)], True)
    copies[5].wait()


def start_kernel(own_ref, other_ref, table_ref, tile_rows_ref, feet_ref, others_ref, out_ref, probes_ref, other_rows_ref):
    half = lax.axis_index("half")
    block_count, probe_count, half_sound = other_ref.shape
    own_at = pl.multiple_of(half * half_sound, LANES)
    other_at = pl.multiple_of((1 - half) * half_sound, LANES)
    probes_ref[:, pl.ds(own_at, half_sound)] = own_ref[...]
    for probe in range(probe_count):
        rows = slice(probe * block_count, (probe + 1) * block_count)
        probes_ref[rows, pl.ds(other_at, half_sound)] = other_ref[:, probe, :]
    square = (block_count, block_count)
    on_diagonal = lax.broadcasted_iota(jnp.int32, square, 0) == lax.broadcasted_iota(
        jnp.int32, square, 1
    )
    others = jnp.where(on_diagonal, jnp.broadcast_to(others_ref[...], square), 0)
    others = jnp.sum(others, axis=1, keepdims=True)
    other_rows_ref[...] = jnp.broadcast_to(others, other_rows_ref.shape)
    pieces = adjoint_pieces(probes_ref[...].astype(jnp.bfloat16), feet_ref)
    table, tile_rows = table_ref[...], tile_rows_ref[...]
    _, lane = tile_iotas()
    data = lax.rem(lane, HALF_LANES) < GROUP
    size = 2 * block_count
    triples = out_ref.shape[0] // (2 * size * probe_count)
    for probe in range(probe_count):
        for triple in range(triples):
            packed = pack_groups(
                [
                    placed_tile(pieces, tile_rows, 3 * triple + part, probe, probe_count)
                    for part in range(3)
                ]
            )
            packed = [jnp.where(data, tile, table) for tile in packed]
            at = 2 * size * (probe * triples + triple)
            for part in range(2):
                out_ref[at + part * size : at + (part + 1) * size, :] = jnp.concatenate(
                    packed[2 * part : 2 * part + 2], axis=0
                ).astype(jnp.bfloat16)


def spatial_build_kernel(left_ref, right_ref, out_ref):
    squared = jnp.maximum(dot(left_ref[...], right_ref[...], ((0,), (0,))), 1e-12)
    distance = squared * lax.rsqrt(squared)
    out_ref[...] = jnp.exp2(distance * (-log2e / kernel_length)).astype(jnp.bfloat16)


def mix(received, choice, temporal):
    periods = temporal.shape[0]
    both = dot(choice, received)
    both = both[: 2 * periods] + both[2 * periods :]
    gathered = both[:periods] + pltpu.roll(both[periods:], HALF_LANES, 1)
    mixed = lax.dot_general(
        gathered * kernel_scale,
        temporal,
        (((0,), (1,)), ((), ())),
        precision=lax.Precision.HIGHEST,
        preferred_element_type=jnp.float32,
    )
    high, low = halves(mixed[:HALF_LANES])

    def columns(part):
        nothing = jnp.zeros(part.shape, part.dtype)
        upper = jnp.concatenate([part, nothing], axis=1)
        return jnp.concatenate([upper, jnp.concatenate([nothing, part], axis=1)], axis=0)

    high, low = columns(high), columns(low)
    upper, lower = choice[: 2 * periods], choice[2 * periods :]
    return (dot(high, upper) + dot(high, lower) + dot(low, upper)).T.astype(jnp.bfloat16)


def first_mix_kernel(top_count, received_ref, temporal_ref, out_ref, choice_ref):
    periods = temporal_ref.shape[0]
    wide = received_ref[...].astype(jnp.float32).T
    shape = (periods, wide.shape[1])
    period = lax.broadcasted_iota(jnp.int32, shape, 0).astype(jnp.float32)
    for column in range(2):
        choice = jnp.zeros(shape, jnp.float32)
        for top in range(top_count):
            at = column * HALF_LANES + GROUP + top
            owner = wide[at : at + 1]
            weight = (
                wide[at + top_count : at + top_count + 1]
                + wide[at + 2 * top_count : at + 2 * top_count + 1]
                + wide[at + 3 * top_count : at + 3 * top_count + 1]
            )
            choice = choice + jnp.where(owner == period, weight, 0.0)
        high, low = halves(choice)
        choice_ref[column * periods : (column + 1) * periods, :] = high
        choice_ref[(2 + column) * periods : (3 + column) * periods, :] = low
    out_ref[...] = mix(received_ref[...], choice_ref[...], temporal_ref[...])


def mix_kernel(received_ref, temporal_ref, choice_ref, out_ref):
    out_ref[...] = mix(received_ref[...], choice_ref[...], temporal_ref[...])


def spatial_kernel(block_count, chunks, streamed, received_ref, tile_rows_ref, other_rows_ref, *refs):
    if streamed:
        own_spatial, other_spatial, out_ref, kept_ref, field, total, sems = refs
    else:
        kept_ref, out_ref, field, total = refs
    rows, half_cells = field.shape
    probe_count = rows // block_count
    tile_count = half_cells // LANES
    copies = []
    if streamed:
        sides = (own_spatial, other_spatial)
        copies = [
            pltpu.make_async_copy(
                sides[side].at[:, start:end], kept_ref.at[side, :, start:end], sems.at[place]
            )
            for place, (side, start, end) in enumerate(chunks)
        ]
        for copy in copies:
            copy.start()
    size = 2 * block_count

    def unpack(probe, carry):
        into = pl.multiple_of(probe * block_count, block_count)
        for triple in range(tile_count // 3):
            at = pl.multiple_of(2 * size * (probe * (tile_count // 3) + triple), size)
            both = received_ref[pl.ds(at, 2 * size), :].astype(jnp.float32)
            packed = [both[part * block_count : (part + 1) * block_count] for part in range(4)]
            for part, value in enumerate(unpack_groups(packed)):
                start = (3 * triple + part) * LANES
                field[pl.ds(into, block_count), start : start + LANES] = value
        return carry

    if streamed:
        lax.fori_loop(0, probe_count, unpack, 0)
    else:
        for pair in range(tile_count * probe_count // 2):
            both = received_ref[size * pair : size * (pair + 1), :].astype(jnp.float32)
            for part in range(2):
                tile, probe = divmod(2 * pair + part, probe_count)
                field[
                    probe * block_count : (probe + 1) * block_count,
                    tile * LANES : (tile + 1) * LANES,
                ] = swap_quarters(both[part * block_count : (part + 1) * block_count])
    cells = field[...].astype(jnp.bfloat16)
    for place, (side, start, end) in enumerate(chunks):
        if streamed:
            copies[place].wait()
        at = side * half_cells
        total[:, at + start : at + end] = dot(cells, kept_ref[side, :, start:end])
    nothing = jnp.zeros((block_count, LANES), jnp.float32)
    for side, rows_ref in enumerate((tile_rows_ref, other_rows_ref)):
        first_tile = rows_ref[...]
        for probe in range(probe_count):
            rows_of = slice(probe * block_count, (probe + 1) * block_count)
            window = [nothing, nothing]
            for tile in range(tile_count):
                at = side * half_cells + tile * LANES
                values = total[rows_of, at : at + LANES]
                for part in range(2):
                    window[part] = jnp.where(first_tile == tile - part, values, window[part])
            for part in range(2):
                at = (2 * side + part) * LANES
                out_ref[rows_of, at : at + LANES] = window[part]


def sound(mine_ref, theirs_ref, feet_ref, other_feet_ref):
    block_count, sound_count, window = feet_ref.shape
    rows = mine_ref.shape[0]
    own = (mine_ref[:, :window] + theirs_ref[:, window:]).astype(jnp.bfloat16)
    other = (mine_ref[:, window:] + theirs_ref[:, :window]).astype(jnp.bfloat16)
    block_index = block_of_row((rows, sound_count), block_count)
    image = jnp.zeros((rows, sound_count), jnp.float32)
    for block in range(block_count):
        part = dot(own, feet_ref[block], ((1,), (1,)))
        part = part + dot(other, other_feet_ref[block], ((1,), (1,)))
        image = jnp.where(block_index == block, part, image)
    return image


def turn_kernel(mine_ref, theirs_ref, feet_ref, other_feet_ref, tile_rows_ref, out_ref, image_ref):
    image = sound(mine_ref, theirs_ref, feet_ref, other_feet_ref)
    image_ref[...] = image
    pieces = adjoint_pieces(image.astype(jnp.bfloat16), feet_ref)
    tile_rows = tile_rows_ref[...]
    size = 2 * feet_ref.shape[0]
    probe_count = image.shape[0] // feet_ref.shape[0]
    count = out_ref.shape[0] // size * 3 // 4
    for pair in range(count):
        tiles = [
            swap_quarters(
                placed_tile(pieces, tile_rows, *divmod(2 * pair + part, probe_count), probe_count)
            )
            for part in range(2)
        ]
        out_ref[size * pair : size * (pair + 1), :] = jnp.concatenate(tiles, axis=0).astype(
            jnp.bfloat16
        )
    out_ref[size * count :, :] = jnp.zeros((out_ref.shape[0] - size * count, LANES), jnp.bfloat16)


def last_kernel(probe_count, mine_ref, theirs_ref, feet_ref, other_feet_ref, probes_ref, first_ref, sums_ref, second_ref):
    second = sound(mine_ref, theirs_ref, feet_ref, other_feet_ref)
    second_ref[...] = second
    probes = probes_ref[...]
    first = first_ref[...]
    block_count = second.shape[0] // probe_count
    lane = lax.broadcasted_iota(jnp.int32, (1, LANES), 1)
    row = jnp.zeros((1, LANES), jnp.float32)
    pairs = (
        (probes, probes),
        (probes, first),
        (first, first),
        (probes, second),
        (first, second),
        (second, second),
    )
    for place, (left, right) in enumerate(pairs):
        product = left * right
        for probe in range(probe_count):
            value = jnp.sum(
                product[probe * block_count : (probe + 1) * block_count], axis=0, keepdims=True
            )
            value = jnp.sum(value, axis=1, keepdims=True)
            row = jnp.where(lane == place * probe_count + probe, value, row)
    sums_ref[...] = jnp.broadcast_to(row, sums_ref.shape)


def finish_kernel(total_rows, sums_ref, probes_ref, first_ref, second_ref, coefficients_ref, residual_ref):
    block_count, probe_count, half_sound = residual_ref.shape
    row = jnp.sum(sums_ref[...], axis=0, keepdims=True) / total_rows

    def stat(place):
        shift = (LANES - place * probe_count) % LANES
        return row if shift == 0 else pltpu.roll(row, shift, 1)

    pp, pw, ww, px, wx, xx = [stat(place) for place in range(6)]
    scale_square = pp + epsilon
    scale = jnp.sqrt(scale_square)
    alpha_one = pw / scale_square
    rest = (ww - 2.0 * alpha_one * pw + alpha_one * alpha_one * pp) / scale_square
    beta_one = jnp.sqrt(jnp.maximum(rest, 0.0) + epsilon)
    cross = wx - alpha_one * ww - alpha_one * px + alpha_one * alpha_one * pw
    alpha_two = (cross / (beta_one * beta_one) - (pw - alpha_one * pp)) / scale_square
    of_second = 1.0 / (scale * beta_one)
    of_first = -(alpha_one + alpha_two) * of_second
    of_probes = (alpha_one * alpha_two / beta_one - beta_one) / scale
    square = (
        of_second * of_second * xx
        + of_first * of_first * ww
        + of_probes * of_probes * pp
        + 2.0 * (of_second * of_first * wx + of_second * of_probes * px + of_first * of_probes * pw)
    )
    beta_two = jnp.sqrt(jnp.maximum(square, 0.0) + epsilon)
    for place, value in enumerate((alpha_one, beta_one, alpha_two, beta_two)):
        coefficients_ref[place : place + 1, :] = value[:, :probe_count]
    at = pl.multiple_of(lax.axis_index("half") * half_sound, LANES)
    for probe in range(probe_count):
        rows = slice(probe * block_count, (probe + 1) * block_count)
        residual_ref[:, probe, :] = (
            of_second[:, probe : probe + 1] * second_ref[rows, pl.ds(at, half_sound)]
            + of_first[:, probe : probe + 1] * first_ref[rows, pl.ds(at, half_sound)]
            + of_probes[:, probe : probe + 1] * probes_ref[rows, pl.ds(at, half_sound)]
        )


def body(probes, footprints, lag_weights, owners, window_tiles, coords, temporal):
    periods = lax.axis_size("period")
    block_count, top_count = owners.shape
    probe_count = probes.shape[1]
    sound_count = footprints.shape[1]
    window = footprints.shape[2]
    cell_count = coords.shape[1]
    half_cells = cell_count // 2
    rows = block_count * probe_count
    total_rows = float(block_count * periods * sound_count)
    f32, bf16 = jnp.float32, jnp.bfloat16
    wire = pltpu.VMEM((periods * HALF_SUBLANES, LANES), bf16)
    vectors = pltpu.VMEM((rows, sound_count), f32)

    def call(kernel, scalars, values, outputs, scratch=(), left_in_hbm=()):
        outputs = tuple(outputs)
        results = pl.pallas_call(
            kernel,
            out_shape=outputs,
            in_specs=[smem] * len(scalars) + [vmem] * len(values) + [hbm] * len(left_in_hbm),
            out_specs=tuple(vmem for _ in outputs),
            scratch_shapes=list(scratch),
            compiler_params=small,
        )(
            *scalars,
            *[in_vmem(value) for value in values],
            *[in_hbm(value) for value in left_in_hbm],
        )
        return results if len(outputs) > 1 else results[0]

    def send(value):
        count = value.shape[0] // periods
        return exchange(value.reshape(periods, count, LANES)).reshape(value.shape)

    def build_spatial(side):
        depth = 256
        return pl.pallas_call(
            spatial_build_kernel,
            out_shape=pltpu.HBM((half_cells, half_cells), bf16),
            grid=(half_cells // depth,),
            in_specs=[
                pl.BlockSpec((16, depth), lambda i: (0, i)),
                pl.BlockSpec((16, half_cells), lambda i: (0, side)),
            ],
            out_specs=pl.BlockSpec((depth, half_cells), lambda i: (i, 0)),
            compiler_params=small,
            name="spatial_build",
        )(in_vmem(left), in_vmem(right))

    chunks = ((0, 0, 1024), (0, 1024, 1536), (1, 0, 512), (1, 512, 1024), (1, 1024, 1536))

    def spatial_step(received, kept):
        scratch = [pltpu.VMEM((rows, half_cells), f32), pltpu.VMEM((rows, cell_count), f32)]
        outputs = [pltpu.VMEM((rows, 2 * window), f32)]
        values, stored = (received, tile_rows, other_rows), ()
        if kept is None:
            outputs.append(pltpu.VMEM((2, half_cells, half_cells), bf16))
            scratch.append(pltpu.SemaphoreType.DMA((len(chunks),)))
            stored = (own_spatial, other_spatial)
        else:
            values = values + (kept,)
        results = call(
            functools.partial(spatial_kernel, block_count, chunks, kept is None),
            (),
            values,
            outputs,
            scratch,
            stored,
        )
        mine, kept = results if kept is None else (results, kept)
        return mine, from_other_half(mine), kept

    tiles = window_tiles.reshape(-1)
    other_probes = from_other_half(probes)
    other_tiles = from_other_half(tiles)
    own_probes, table, tile_rows, left, right, first_feet = call(
        prepare_kernel,
        (),
        (),
        (
            pltpu.VMEM((rows, sound_count // 2), f32),
            pltpu.VMEM((2 * HALF_SUBLANES, LANES), f32),
            pltpu.VMEM((2 * HALF_SUBLANES, LANES), jnp.int32),
            pltpu.VMEM((16, half_cells), bf16),
            pltpu.VMEM((16, cell_count), bf16),
            pltpu.VMEM(footprints.shape, bf16),
        ),
        (
            pltpu.SMEM(tiles.shape, jnp.int32),
            pltpu.SMEM((top_count, block_count), jnp.int32),
            pltpu.SMEM((top_count, block_count), f32),
            pltpu.VMEM(probes.shape, f32),
            pltpu.VMEM(coords.shape, jnp.int32),
            pltpu.SemaphoreType.DMA((6,)),
        ),
        (tiles, owners.T, lag_weights.T, probes, coords, footprints),
    )
    to_mix, all_probes, other_rows = call(
        start_kernel,
        (),
        (own_probes, other_probes, table, tile_rows, first_feet, other_tiles.reshape(1, -1)),
        (wire, vectors, pltpu.VMEM((block_count, LANES), jnp.int32)),
    )
    received = send(to_mix)
    other_feet = from_other_half(footprints)
    own_spatial = build_spatial(0)
    received, own_spatial = lax.optimization_barrier((received, own_spatial))
    mixed, choice = call(
        functools.partial(first_mix_kernel, top_count),
        (),
        (received, temporal),
        (wire, pltpu.VMEM((4 * periods, periods * HALF_SUBLANES), bf16)),
    )
    other_spatial = build_spatial(1)
    mine, theirs, kept = spatial_step(send(mixed), None)
    to_mix, first = call(
        turn_kernel, (), (mine, theirs, footprints, other_feet, tile_rows), (wire, vectors)
    )
    mixed = call(mix_kernel, (), (send(to_mix), temporal, choice), (wire,))
    mine, theirs, kept = spatial_step(send(mixed), kept)
    sums, second = call(
        functools.partial(last_kernel, probe_count),
        (),
        (mine, theirs, footprints, other_feet, all_probes, first),
        (pltpu.VMEM((periods, LANES), f32), vectors),
    )
    sums = exchange(sums.reshape(periods, 1, LANES)).reshape(periods, LANES)
    return pl.pallas_call(
        functools.partial(finish_kernel, total_rows),
        out_shape=(
            jax.ShapeDtypeStruct((4, probe_count), f32),
            jax.ShapeDtypeStruct(probes.shape, f32),
        ),
        in_specs=[vmem, vmem, vmem, vmem],
        out_specs=(vmem, vmem),
        compiler_params=small,
        name="finish",
    )(in_vmem(sums), in_vmem(all_probes), in_vmem(first), in_vmem(second))


def solution(mesh):
    in_specs = (
        P("period", None, "half"),
        P("period", None, "half"),
        P("period", None),
        P("period", None),
        P("period", "half"),
        P(),
        P(),
    )
    out_specs = (P(), P("period", None, "half"))
    return jax.shard_map(body, mesh=mesh, in_specs=in_specs, out_specs=out_specs, check_vma=False)
```

profile of v0, /device:TPU:1, one launch (start us, length us, event | category | flops | bytes accessed | tf_op | source)
XLA Modules:
  0.0 124.0 jit_solution(7807899503664645441)
XLA Ops:
  0.6 3.3 %collective-permute-start.3 = (bf16[8,512,256]{2,1,0:T(8,128)(2,1)}, bf16[8,512,256]{2,1,0:T(8,128)(2,1)S(1)}, u32[]{:S(2)}, u32[]{:S(2)}) collective-permute-start(bf16[8,512,256]{2,1,0:T(8,128)(2,1)} %feet_ref.3), channel_id=1, source_target_pairs={{0,1},{1,0},{2,3},{3,2},{4,5},{5,4},{6,7},{7,6},{8,9},{9,8},{10,11... | collective-permute-start | bytes 6291464 | tf_op jit(solution)/shard_map/ppermute | solution.py:36
  4.4 1.7 %shard_map.86 = (f32[32,256]{1,0:T(8,128)S(1)}, f32[8,128]{1,0:T(8,128)S(1)}, s32[8,128]{1,0:T(8,128)S(1)}, bf16[16,1536]{1,0:T(8,128)(2,1)S(1)}, bf16[16,3072]{...) custom-call(s32[8]{0:T(128)} %bitcast.28, s32[4,8]{1,0:T(4,128)} %bitcast.25, f32[4,8]{1,0:T(4,128)} %bitcast.26, ...), custom_call_target="tpu_custom_call" | custom-call | tf_op jit(solution)/shard_map/pallas_call | solution.py:477
  6.2 1.8 %collective-permute-done.1 = s32[8]{0:T(128)S(1)} collective-permute-done((s32[8]{0:T(128)}, s32[8]{0:T(128)S(1)}, u32[]{:S(2)}, u32[]{:S(2)}) %collective-permute-start.1) | collective-permute-done | bytes 64 | tf_op jit(solution)/shard_map/ppermute | solution.py:36
  8.0 1.3 %shard_map.87 = (bf16[512,128]{1,0:T(8,128)(2,1)}, f32[32,512]{1,0:T(8,128)S(1)}, s32[8,128]{1,0:T(8,128)S(1)}) custom-call(f32[32,256]{1,0:T(8,128)S(1)} %get-tuple-element.21.own_ref, f32[8,4,256]{2,1,0:T(4,128)S(1)} %collective-permute-done.other_ref, f32[8,128]{1,0:T(8,128)S(1)} %get-tuple-element.22.table_ref, ...), custom_call_target="tpu_custom_call" | custom-call | tf_op jit(solution)/shard_map/pallas_call | solution.py:477
  9.3 13.8 %all-to-all-start = ((bf16[128,4,128]{2,1,0:T(4,128)(2,1)}), bf16[128,4,128]{2,1,0:T(4,128)(2,1)S(1)}, u32[]{:S(2)}, u32[]{:S(2)}) async-start(bf16[128,4,128]{2,1,0:T(4,128)(2,1)} %bitcast.4), calls=%async_computation | async-start | bytes 262144 | tf_op jit(solution)/shard_map/all_to_all | solution.py:40
  23.1 5.2 %spatial_build.2.refs_0_ = bf16[1536,1536]{1,0:T(8,128)(2,1)} custom-call(bf16[16,1536]{1,0:T(8,128)(2,1)S(1)} %get-tuple-element.26.left_ref, bf16[16,3072]{1,0:T(8,128)(2,1)S(1)} %get-tuple-element.27.right_ref), custom_call_target="tpu_custom_call" | custom-call | tf_op jit(solution)/shard_map/spatial_build/pallas_call | solution.py:497
  28.3 6.0 %all-to-all-done = bf16[128,4,128]{2,1,0:T(4,128)(2,1)S(1)} async-done(((bf16[128,4,128]{2,1,0:T(4,128)(2,1)}), bf16[128,4,128]{2,1,0:T(4,128)(2,1)S(1)}, u32[]{:S(2)}, u32[]{:S(2)}) %all-to-all-start) | async-done | bytes 131104 | tf_op jit(solution)/shard_map/all_to_all | solution.py:40
  34.3 1.9 %shard_map.88 = (bf16[512,128]{1,0:T(8,128)(2,1)}, bf16[512,512]{1,0:T(8,128)(2,1)S(1)}) custom-call(bf16[512,128]{1,0:T(8,128)(2,1)S(1)} %bitcast.18, f32[128,128]{1,0:T(8,128)S(1)} %copy-done.1), custom_call_target="tpu_custom_call" | custom-call | tf_op jit(solution)/shard_map/pallas_call | solution.py:477
  36.2 7.2 %all-to-all-start.1 = ((bf16[128,4,128]{2,1,0:T(4,128)(2,1)}), bf16[128,4,128]{2,1,0:T(4,128)(2,1)S(1)}, u32[]{:S(2)}, u32[]{:S(2)}) async-start(bf16[128,4,128]{2,1,0:T(4,128)(2,1)} %bitcast.6), calls=%async_computation.1 | async-start | bytes 262144 | tf_op jit(solution)/shard_map/all_to_all | solution.py:40
  43.4 5.2 %spatial_build.3.refs_1_ = bf16[1536,1536]{1,0:T(8,128)(2,1)} custom-call(bf16[16,1536]{1,0:T(8,128)(2,1)S(1)} %get-tuple-element.26.left_ref, bf16[16,3072]{1,0:T(8,128)(2,1)S(1)} %get-tuple-element.27.right_ref), custom_call_target="tpu_custom_call" | custom-call | tf_op jit(solution)/shard_map/spatial_build/pallas_call | solution.py:497
  48.6 6.0 %all-to-all-done.1 = bf16[128,4,128]{2,1,0:T(4,128)(2,1)S(1)} async-done(((bf16[128,4,128]{2,1,0:T(4,128)(2,1)}), bf16[128,4,128]{2,1,0:T(4,128)(2,1)S(1)}, u32[]{:S(2)}, u32[]{:S(2)}) %all-to-all-start.1) | async-done | bytes 131104 | tf_op jit(solution)/shard_map/all_to_all | solution.py:40
  54.6 4.3 %shard_map.89 = (f32[32,512]{1,0:T(8,128)S(1)}, bf16[2,1536,1536]{2,1,0:T(8,128)(2,1)S(1)}) custom-call(bf16[512,128]{1,0:T(8,128)(2,1)S(1)} %bitcast.16, s32[8,128]{1,0:T(8,128)S(1)} %get-tuple-element.23.tile_rows_ref, s32[8,128]{1,0:T(8,128)S(1)} %get-tuple-element.30.other_rows_ref, bf16[1536,1536]{1,0:T(8,128)(2,1)} %spatial_build.2.refs_0_, ...), custom_call_target="tpu_custom_call" | custom-call | tf_op jit(solution)/shard_map/pallas_call | solution.py:477
  58.9 2.5 %collective-permute-start.2 = (f32[32,512]{1,0:T(8,128)S(1)}, f32[32,512]{1,0:T(8,128)S(1)}, u32[]{:S(2)}, u32[]{:S(2)}) collective-permute-start(f32[32,512]{1,0:T(8,128)S(1)} %get-tuple-element.32.mine_ref), channel_id=1, source_target_pairs={{0,1},{1,0},{2,3},{3,2},{4,5},{5,4},{6,7},{7,6},{8,9},{9,8},{10,11... | collective-permute-start | bytes 196616 | tf_op jit(solution)/shard_map/ppermute | solution.py:36
  61.4 0.9 collective-permute-done.2.theirs_ref
  62.3 1.9 %shard_map.90 = (bf16[512,128]{1,0:T(8,128)(2,1)S(1)}, f32[32,512]{1,0:T(8,128)S(1)}) custom-call(f32[32,512]{1,0:T(8,128)S(1)} %get-tuple-element.32.mine_ref, f32[32,512]{1,0:T(8,128)S(1)} %collective-permute-done.2.theirs_ref, bf16[8,512,256]{2,1,0:T(8,128)(2,1)S(1)} %copy-done, bf16[8,512,256]{2,1,0:T(8,128)(2,1)S(1)} %collective-permute-done.3.other_feet_ref, ...), custom_call_target="tpu_custom_call" | custom-call | tf_op jit(solution)/shard_map/pallas_call | solution.py:477
  64.2 17.4 %all_to_all.25 = bf16[128,4,128]{2,1,0:T(4,128)(2,1)S(1)} all-to-all(bf16[128,4,128]{2,1,0:T(4,128)(2,1)S(1)} %bitcast.22), channel_id=1, replica_groups=mesh['period'=128,'half'=2] {'period'}, dimensions={0} | all-to-all | bytes 262144 | tf_op jit(solution)/shard_map/all_to_all | solution.py:40
  81.6 1.1 shard_map.91
  82.7 16.8 %all_to_all.26 = bf16[128,4,128]{2,1,0:T(4,128)(2,1)S(1)} all-to-all(bf16[128,4,128]{2,1,0:T(4,128)(2,1)S(1)} %bitcast.20), channel_id=1, replica_groups=mesh['period'=128,'half'=2] {'period'}, dimensions={0} | all-to-all | bytes 262144 | tf_op jit(solution)/shard_map/all_to_all | solution.py:40
  99.5 1.8 %shard_map.92.mine_ref = f32[32,512]{1,0:T(8,128)S(1)} custom-call(bf16[512,128]{1,0:T(8,128)(2,1)S(1)} %bitcast.17, s32[8,128]{1,0:T(8,128)S(1)} %get-tuple-element.23.tile_rows_ref, s32[8,128]{1,0:T(8,128)S(1)} %get-tuple-element.30.other_rows_ref, bf16[2,1536,1536]{2,1,0:T(8,128)(2,1)S(1)} %get-tuple-element.35.refs_0_), custom_call_target="tpu_custom_call" | custom-call | tf_op jit(solution)/shard_map/pallas_call | solution.py:477
  101.3 3.2 %collective-permute-start.4 = (f32[32,512]{1,0:T(8,128)S(1)}, f32[32,512]{1,0:T(8,128)S(1)}, u32[]{:S(2)}, u32[]{:S(2)}) collective-permute-start(f32[32,512]{1,0:T(8,128)S(1)} %shard_map.92.mine_ref), channel_id=1, source_target_pairs={{0,1},{1,0},{2,3},{3,2},{4,5},{5,4},{6,7},{7,6},{8,9},{9,8},{10,11... | collective-permute-start | bytes 196616 | tf_op jit(solution)/shard_map/ppermute | solution.py:36
  104.5 0.9 collective-permute-done.4.theirs_ref
  105.4 1.5 %shard_map.93 = (f32[128,128]{1,0:T(8,128)S(1)}, f32[32,512]{1,0:T(8,128)S(1)}) custom-call(f32[32,512]{1,0:T(8,128)S(1)} %shard_map.92.mine_ref, f32[32,512]{1,0:T(8,128)S(1)} %collective-permute-done.4.theirs_ref, bf16[8,512,256]{2,1,0:T(8,128)(2,1)S(1)} %copy-done, bf16[8,512,256]{2,1,0:T(8,128)(2,1)S(1)} %collective-permute-done.3.other_feet_ref, ...), custom_call_target="tpu_custom_call" | custom-call | tf_op jit(solution)/shard_map/pallas_call | solution.py:477
  106.8 16.3 %all_to_all.27 = f32[128,1,128]{2,1,0:T(1,128)S(1)} all-to-all(f32[128,1,128]{2,1,0:T(1,128)S(1)} %bitcast.23), channel_id=1, replica_groups=mesh['period'=128,'half'=2] {'period'}, dimensions={0} | all-to-all | bytes 131072 | tf_op jit(solution)/shard_map/all_to_all | solution.py:40
  123.1 0.9 finish.1
  (8 shorter events, 0.5 us)
Async XLA Ops:
  0.6 61.7 %collective-permute-start.3 = (bf16[8,512,256]{2,1,0:T(8,128)(2,1)}, bf16[8,512,256]{2,1,0:T(8,128)(2,1)S(1)}, u32[]{:S(2)}, u32[]{:S(2)}) collective-permute-start(bf16[8,512,256]{2,1,0:T(8,128)(2,1)} %feet_ref.3), channel_id=1, source_target_pairs={{0,1},{1,0},{2,3},{3,2},{4,5},{5,4},{6,7},{7,6},{8,9},{9,8},{10,11... | collective-permute-start | bytes 6291464 | tf_op jit(solution)/shard_map/ppermute | solution.py:36
  3.9 4.0 %collective-permute-start = (f32[8,4,256]{2,1,0:T(4,128)}, f32[8,4,256]{2,1,0:T(4,128)S(1)}, u32[]{:S(2)}, u32[]{:S(2)}) collective-permute-start(f32[8,4,256]{2,1,0:T(4,128)} %own_in.1), channel_id=1, source_target_pairs={{0,1},{1,0},{2,3},{3,2},{4,5},{5,4},{6,7},{7,6},{8,9},{9,8},{10,11... | collective-permute-start | bytes 98312 | tf_op jit(solution)/shard_map/ppermute | solution.py:36
  4.0 3.9 %collective-permute-start.1 = (s32[8]{0:T(128)}, s32[8]{0:T(128)S(1)}, u32[]{:S(2)}, u32[]{:S(2)}) collective-permute-start(s32[8]{0:T(128)} %bitcast.27), channel_id=1, source_target_pairs={{0,1},{1,0},{2,3},{3,2},{4,5},{5,4},{6,7},{7,6},{8,9},{9,8},{10,11... | collective-permute-start | bytes 104 | tf_op jit(solution)/shard_map/ppermute | solution.py:36
  4.4 29.8 %copy-start.1 = (f32[128,128]{1,0:T(8,128)S(1)}, f32[128,128]{1,0:T(8,128)}, u32[]{:S(2)}) copy-start(f32[128,128]{1,0:T(8,128)} %temporal_ref.3) | copy-start | bytes 196612
  9.3 25.0 %all-to-all-start = ((bf16[128,4,128]{2,1,0:T(4,128)(2,1)}), bf16[128,4,128]{2,1,0:T(4,128)(2,1)S(1)}, u32[]{:S(2)}, u32[]{:S(2)}) async-start(bf16[128,4,128]{2,1,0:T(4,128)(2,1)} %bitcast.4), calls=%async_computation | async-start | bytes 262144 | tf_op jit(solution)/shard_map/all_to_all | solution.py:40
  36.2 18.4 %all-to-all-start.1 = ((bf16[128,4,128]{2,1,0:T(4,128)(2,1)}), bf16[128,4,128]{2,1,0:T(4,128)(2,1)S(1)}, u32[]{:S(2)}, u32[]{:S(2)}) async-start(bf16[128,4,128]{2,1,0:T(4,128)(2,1)} %bitcast.6), calls=%async_computation.1 | async-start | bytes 262144 | tf_op jit(solution)/shard_map/all_to_all | solution.py:40
  54.6 7.7 %copy-start = (bf16[8,512,256]{2,1,0:T(8,128)(2,1)S(1)}, bf16[8,512,256]{2,1,0:T(8,128)(2,1)}, u32[]{:S(2)}) copy-start(bf16[8,512,256]{2,1,0:T(8,128)(2,1)} %feet_ref.3) | copy-start | bytes 6291460
  58.9 3.4 %collective-permute-start.2 = (f32[32,512]{1,0:T(8,128)S(1)}, f32[32,512]{1,0:T(8,128)S(1)}, u32[]{:S(2)}, u32[]{:S(2)}) collective-permute-start(f32[32,512]{1,0:T(8,128)S(1)} %get-tuple-element.32.mine_ref), channel_id=1, source_target_pairs={{0,1},{1,0},{2,3},{3,2},{4,5},{5,4},{6,7},{7,6},{8,9},{9,8},{10,11... | collective-permute-start | bytes 196616 | tf_op jit(solution)/shard_map/ppermute | solution.py:36
  101.3 4.1 %collective-permute-start.4 = (f32[32,512]{1,0:T(8,128)S(1)}, f32[32,512]{1,0:T(8,128)S(1)}, u32[]{:S(2)}, u32[]{:S(2)}) collective-permute-start(f32[32,512]{1,0:T(8,128)S(1)} %shard_map.92.mine_ref), channel_id=1, source_target_pairs={{0,1},{1,0},{2,3},{3,2},{4,5},{5,4},{6,7},{7,6},{8,9},{9,8},{10,11... | collective-permute-start | bytes 196616 | tf_op jit(solution)/shard_map/ppermute | solution.py:36
where the time goes:
time: 124 us
  blocking collectives  50.5 us (41%)
  starting transfers between devices  30.5 us (25%)
  Pallas kernels  26.8 us (22%)
  waiting for transfers between devices  15.6 us (13%)
    all_to_all x3, blocking collectives, exchange(): lax.all_to_all(value, 'period', split_axis=0, concat_axis=0, tiled=True)  50.5 us
    all_to_all x2, starting transfers between devices, exchange(): lax.all_to_all(value, 'period', split_axis=0, concat_axis=0, tiled=True)  21 us
    pallas_call x8, Pallas kernels, call(): pl.pallas_call(kernel, out_shape=outputs, in_specs=[smem] * len(scalars)...  15.5 us
    all_to_all x2, waiting for transfers between devices, exchange(): lax.all_to_all(value, 'period', split_axis=0, concat_axis=0, tiled=True)  12 us
    pallas_call x2, Pallas kernels, build_spatial(): pl.pallas_call(spatial_build_kernel, out_shape=pltpu.HBM((half_cells, hal...  10.4 us
    ppermute x5, starting transfers between devices, from_other_half(): return lax.ppermute(value, 'half', [(0, 1), (1, 0)])  9.48 us
    ppermute x5, waiting for transfers between devices, from_other_half(): return lax.ppermute(value, 'half', [(0, 1), (1, 0)])  3.62 us
  transfers between devices with their start and end apart: 7, of which 5 were waited for; matrix products, arithmetic and copies ran while one was open for 0% of the time, Pallas kernels for 16%

commit v1 on v0

--- a/solution.py
+++ b/solution.py
@@ -178,12 +178,7 @@
             here = here & (lax.rem(row, HALF_SUBLANES) == turn)
             owner = jnp.where(here, owners_ref[top, block].astype(jnp.float32), owner)
             weight = jnp.where(here, weights_ref[top, block], weight)
-    table = owner
-    for part in range(1, 4):
-        high = weight.astype(jnp.bfloat16).astype(jnp.float32)
-        table = table + pltpu.roll(high, part * top_count, 1)
-        weight = weight - high
-    table_ref[...] = table
+    table_ref[...] = owner + pltpu.roll(weight, top_count, 1)
     tile_rows = jnp.zeros(row.shape, jnp.int32)
     for block in range(block_count):
         tile_rows = jnp.where(row == block, tiles_ref[block], tile_rows)
@@ -237,34 +232,50 @@
                 ).astype(jnp.bfloat16)
 
 
-def spatial_build_kernel(left_ref, right_ref, out_ref):
-    squared = jnp.maximum(dot(left_ref[...], right_ref[...], ((0,), (0,))), 1e-12)
+def spatial_values(left, right):
+    squared = jnp.maximum(dot(left, right, ((0,), (0,))), 1e-12)
     distance = squared * lax.rsqrt(squared)
-    out_ref[...] = jnp.exp2(distance * (-log2e / kernel_length)).astype(jnp.bfloat16)
+    return jnp.exp2(distance * (-log2e / kernel_length)).astype(jnp.bfloat16)
+
+
+def first_build_kernel(left_ref, right_ref, own_out, top_out, buffers, sems):
+    half_cells = left_ref.shape[1]
+    depth = buffers.shape[1]
+    count = half_cells // depth
+    copies = []
+    for place in range(count + 1):
+        at = depth * (place % count)
+        if place < count:
+            right = right_ref[:, at:half_cells]
+            target = own_out.at[at : at + depth, at:]
+        else:
+            right = right_ref[:, half_cells:]
+            target = top_out
+        buffers[place, :, at:] = spatial_values(left_ref[:, at : at + depth], right)
+        copy = pltpu.make_async_copy(buffers.at[place, :, at:], target, sems.at[place])
+        copy.start()
+        copies.append(copy)
+    for copy in copies:
+        copy.wait()
+
+
+def second_build_kernel(left_ref, right_ref, out_ref):
+    out_ref[...] = spatial_values(left_ref[...], right_ref[...])
 
 
 def mix(received, choice, temporal):
     periods = temporal.shape[0]
     both = dot(choice, received)
-    both = both[: 2 * periods] + both[2 * periods :]
     gathered = both[:periods] + pltpu.roll(both[periods:], HALF_LANES, 1)
-    mixed = lax.dot_general(
-        gathered * kernel_scale,
-        temporal,
-        (((0,), (1,)), ((), ())),
-        precision=lax.Precision.HIGHEST,
-        preferred_element_type=jnp.float32,
-    )
-    high, low = halves(mixed[:HALF_LANES])
-
-    def columns(part):
-        nothing = jnp.zeros(part.shape, part.dtype)
-        upper = jnp.concatenate([part, nothing], axis=1)
-        return jnp.concatenate([upper, jnp.concatenate([nothing, part], axis=1)], axis=0)
-
-    high, low = columns(high), columns(low)
-    upper, lower = choice[: 2 * periods], choice[2 * periods :]
-    return (dot(high, upper) + dot(high, lower) + dot(low, upper)).T.astype(jnp.bfloat16)
+    high, low = halves(gathered * kernel_scale)
+    temporal_high, temporal_low = halves(temporal)
+    turned = ((0,), (1,))
+    mixed = dot(high, temporal_high, turned) + dot(high, temporal_low, turned)
+    mixed = (mixed + dot(low, temporal_high, turned))[:HALF_LANES].astype(jnp.bfloat16)
+    nothing = jnp.zeros(mixed.shape, jnp.bfloat16)
+    upper = jnp.concatenate([mixed, nothing], axis=1)
+    lower = jnp.concatenate([nothing, mixed], axis=1)
+    return dot(jnp.concatenate([upper, lower], axis=0), choice).T.astype(jnp.bfloat16)
 
 
 def first_mix_kernel(top_count, received_ref, temporal_ref, out_ref, choice_ref):
@@ -276,16 +287,9 @@
         choice = jnp.zeros(shape, jnp.float32)
         for top in range(top_count):
             at = column * HALF_LANES + GROUP + top
-            owner = wide[at : at + 1]
-            weight = (
-                wide[at + top_count : at + top_count + 1]
-                + wide[at + 2 * top_count : at + 2 * top_count + 1]
-                + wide[at + 3 * top_count : at + 3 * top_count + 1]
-            )
-            choice = choice + jnp.where(owner == period, weight, 0.0)
-        high, low = halves(choice)
-        choice_ref[column * periods : (column + 1) * periods, :] = high
-        choice_ref[(2 + column) * periods : (3 + column) * periods, :] = low
+            weight = wide[at + top_count : at + top_count + 1]
+            choice = jnp.where(wide[at : at + 1] == period, weight, choice)
+        choice_ref[column * periods : (column + 1) * periods, :] = choice.astype(jnp.bfloat16)
     out_ref[...] = mix(received_ref[...], choice_ref[...], temporal_ref[...])
 
 
@@ -293,25 +297,33 @@
     out_ref[...] = mix(received_ref[...], choice_ref[...], temporal_ref[...])
 
 
-def spatial_kernel(block_count, chunks, streamed, received_ref, tile_rows_ref, other_rows_ref, *refs):
+def spatial_kernel(block_count, depth, width, streamed, received_ref, tile_rows_ref, other_rows_ref, *refs):
     if streamed:
-        own_spatial, other_spatial, out_ref, kept_ref, field, total, sems = refs
+        own_in, top_in, rest_in, feet_in, out_ref, kept_ref, feet_ref, field, total, sems = refs
     else:
         kept_ref, out_ref, field, total = refs
     rows, half_cells = field.shape
     probe_count = rows // block_count
     tile_count = half_cells // LANES
-    copies = []
+    own_copies, other_copies = [], []
     if streamed:
-        sides = (own_spatial, other_spatial)
+        pairs = [
+            (own_in.at[at : at + depth, at:], kept_ref.at[0, at : at + depth, at:])
+            for at in range(0, half_cells, depth)
+        ]
+        for at in range(0, half_cells, width):
+            columns = slice(at, at + width)
+            pairs.append((top_in.at[:, columns], kept_ref.at[1, :depth, columns]))
+            pairs.append((rest_in.at[:, columns], kept_ref.at[1, depth:, columns]))
+        pairs.append((feet_in, feet_ref))
         copies = [
-            pltpu.make_async_copy(
-                sides[side].at[:, start:end], kept_ref.at[side, :, start:end], sems.at[place]
-            )
-            for place, (side, start, end) in enumerate(chunks)
+            pltpu.make_async_copy(source, target, sems.at[place])
+            for place, (source, target) in enumerate(pairs)
         ]
         for copy in copies:
             copy.start()
+        own_copies, other_copies = copies[: half_cells // depth], copies[half_cells // depth :]
+        feet_copy = copies[-1]
     size = 2 * block_count
 
     def unpack(probe, carry):
@@ -337,11 +349,19 @@
                     tile * LANES : (tile + 1) * LANES,
                 ] = swap_quarters(both[part * block_count : (part + 1) * block_count])
     cells = field[...].astype(jnp.bfloat16)
-    for place, (side, start, end) in enumerate(chunks):
-        if streamed:
-            copies[place].wait()
-        at = side * half_cells
-        total[:, at + start : at + end] = dot(cells, kept_ref[side, :, start:end])
+    for copy in own_copies:
+        copy.wait()
+    for at in range(0, half_cells, depth):
+        end = at + depth
+        value = dot(cells[:, :end], kept_ref[0, :end, at:end])
+        if end < half_cells:
+            value = value + dot(cells[:, end:], kept_ref[0, at:end, end:], ((1,), (1,)))
+        total[:, at:end] = value
+    for place, at in enumerate(range(0, half_cells, width)):
+        for copy in other_copies[2 * place : 2 * place + 2]:
+            copy.wait()
+        start = half_cells + at
+        total[:, start : start + width] = dot(cells, kept_ref[1, :, at : at + width])
     nothing = jnp.zeros((block_count, LANES), jnp.float32)
     for side, rows_ref in enumerate((tile_rows_ref, other_rows_ref)):
         first_tile = rows_ref[...]
@@ -356,6 +376,8 @@
             for part in range(2):
                 at = (2 * side + part) * LANES
                 out_ref[rows_of, at : at + LANES] = window[part]
+    if streamed:
+        feet_copy.wait()
 
 
 def sound(mine_ref, theirs_ref, feet_ref, other_feet_ref):
@@ -492,22 +514,39 @@
         count = value.shape[0] // periods
         return exchange(value.reshape(periods, count, LANES)).reshape(value.shape)
 
-    def build_spatial(side):
-        depth = 256
+    depth, width = 256, 512
+    block_rows = half_cells // depth
+
+    def first_build():
         return pl.pallas_call(
-            spatial_build_kernel,
-            out_shape=pltpu.HBM((half_cells, half_cells), bf16),
-            grid=(half_cells // depth,),
+            first_build_kernel,
+            out_shape=(
+                pltpu.HBM((half_cells, half_cells), bf16),
+                pltpu.HBM((depth, half_cells), bf16),
+            ),
+            in_specs=[vmem, vmem],
+            out_specs=(hbm, hbm),
+            scratch_shapes=[
+                pltpu.VMEM((block_rows + 1, depth, half_cells), bf16),
+                pltpu.SemaphoreType.DMA((block_rows + 1,)),
+            ],
+            compiler_params=small,
+            name="first_build",
+        )(in_vmem(left), in_vmem(right))
+
+    def second_build():
+        return pl.pallas_call(
+            second_build_kernel,
+            out_shape=pltpu.HBM((half_cells - depth, half_cells), bf16),
+            grid=(block_rows - 1,),
             in_specs=[
-                pl.BlockSpec((16, depth), lambda i: (0, i)),
-                pl.BlockSpec((16, half_cells), lambda i: (0, side)),
+                pl.BlockSpec((16, depth), lambda i: (0, i + 1)),
+                pl.BlockSpec((16, half_cells), lambda i: (0, 1)),
             ],
             out_specs=pl.BlockSpec((depth, half_cells), lambda i: (i, 0)),
             compiler_params=small,
-            name="spatial_build",
+            name="second_build",
         )(in_vmem(left), in_vmem(right))
-
-    chunks = ((0, 0, 1024), (0, 1024, 1536), (1, 0, 512), (1, 512, 1024), (1, 1024, 1536))
 
     def spatial_step(received, kept):
         scratch = [pltpu.VMEM((rows, half_cells), f32), pltpu.VMEM((rows, cell_count), f32)]
@@ -515,20 +554,24 @@
         values, stored = (received, tile_rows, other_rows), ()
         if kept is None:
             outputs.append(pltpu.VMEM((2, half_cells, half_cells), bf16))
-            scratch.append(pltpu.SemaphoreType.DMA((len(chunks),)))
-            stored = (own_spatial, other_spatial)
+            outputs.append(pltpu.VMEM(footprints.shape, bf16))
+            count = block_rows + 2 * half_cells // width + 1
+            scratch.append(pltpu.SemaphoreType.DMA((count,)))
+            stored = (own_spatial, top_spatial, rest_spatial, other_feet)
         else:
             values = values + (kept,)
         results = call(
-            functools.partial(spatial_kernel, block_count, chunks, kept is None),
+            functools.partial(spatial_kernel, block_count, depth, width, kept is None),
             (),
             values,
             outputs,
             scratch,
             stored,
         )
-        mine, kept = results if kept is None else (results, kept)
-        return mine, from_other_half(mine), kept
+        if kept is None:
+            mine, kept, feet = results
+            return mine, from_other_half(mine), kept, feet
+        return results, from_other_half(results)
 
     tiles = window_tiles.reshape(-1)
     other_probes = from_other_half(probes)
@@ -563,21 +606,23 @@
     )
     received = send(to_mix)
     other_feet = from_other_half(footprints)
-    own_spatial = build_spatial(0)
-    received, own_spatial = lax.optimization_barrier((received, own_spatial))
+    own_spatial, top_spatial = first_build()
+    received, own_spatial, top_spatial = lax.optimization_barrier(
+        (received, own_spatial, top_spatial)
+    )
     mixed, choice = call(
         functools.partial(first_mix_kernel, top_count),
         (),
         (received, temporal),
-        (wire, pltpu.VMEM((4 * periods, periods * HALF_SUBLANES), bf16)),
-    )
-    other_spatial = build_spatial(1)
-    mine, theirs, kept = spatial_step(send(mixed), None)
+        (wire, pltpu.VMEM((2 * periods, periods * HALF_SUBLANES), bf16)),
+    )
+    rest_spatial = second_build()
+    mine, theirs, kept, other_feet = spatial_step(send(mixed), None)
     to_mix, first = call(
         turn_kernel, (), (mine, theirs, footprints, other_feet, tile_rows), (wire, vectors)
     )
     mixed = call(mix_kernel, (), (send(to_mix), temporal, choice), (wire,))
-    mine, theirs, kept = spatial_step(send(mixed), kept)
+    mine, theirs = spatial_step(send(mixed), kept)
     sums, second = call(
         functools.partial(last_kernel, probe_count),
         (),

time: 124 us -> 125 us (level)
  Pallas kernels: 26.8 us -> 23.4 us
  waiting for transfers between devices: 15.6 us -> 18.3 us
  local copies, waits for them, and re-layouts: 0.01 us -> 1.38 us
    pallas_call x2, Pallas kernels: 10.4 us -> 7.73 us  [the longest x1 4.64 us: second_build(): pl.pallas_call(second_build_kernel, out_shape=pltpu.HBM((half_cells - dep...]
    all_to_all x2, waiting for transfers between devices: 12 us -> 14.6 us  [exchange(): lax.all_to_all(value, 'period', split_axis=0, concat_axis=0, tiled=True)]
    unnamed x4 -> x6, local copies, waits for them, and re-layouts: 0.01 us -> 1.38 us
  transfers between devices with their start and end apart: 7 -> 7, of which waited for: 5 -> 5; matrix products, arithmetic and copies ran while one was open for 0% -> 0% of each run, Pallas kernels for 16% -> 10%
where the time goes in v1:
time: 125 us; the launch traced here: 124 us
  blocking collectives  50 us (40%)
  starting transfers between devices  30.4 us (24%)
  Pallas kernels  23.4 us (19%)
  waiting for transfers between devices  18.3 us (15%)
  local copies, waits for them, and re-layouts  1.38 us (1%)
    all_to_all x3, blocking collectives, exchange(): lax.all_to_all(value, 'period', split_axis=0, concat_axis=0, tiled=True)  50 us
    all_to_all x2, starting transfers between devices, exchange(): lax.all_to_all(value, 'period', split_axis=0, concat_axis=0, tiled=True)  20 us
    pallas_call x8, Pallas kernels, call(): pl.pallas_call(kernel, out_shape=outputs, in_specs=[smem] * len(scalars)...  14.8 us
    all_to_all x2, waiting for transfers between devices, exchange(): lax.all_to_all(value, 'period', split_axis=0, concat_axis=0, tiled=True)  14.6 us
    ppermute x5, starting transfers between devices, from_other_half(): return lax.ppermute(value, 'half', [(0, 1), (1, 0)])  10.4 us
    pallas_call x1, Pallas kernels, second_build(): pl.pallas_call(second_build_kernel, out_shape=pltpu.HBM((half_cells - dep...  4.64 us
    ppermute x5, waiting for transfers between devices, from_other_half(): return lax.ppermute(value, 'half', [(0, 1), (1, 0)])  3.62 us
    pallas_call x1, Pallas kernels, first_build(): pl.pallas_call(first_build_kernel, out_shape=(pltpu.HBM((half_cells, half...  3.08 us
  transfers between devices with their start and end apart: 7, of which 5 were waited for; matrix products, arithmetic and copies ran while one was open for 0% of the time, Pallas kernels for 10%

profile of v1, /device:TPU:1, one launch (start us, length us, event | category | flops | bytes accessed | tf_op | source)
XLA Modules:
  0.0 124.2 jit_solution(15031216158265039829)
XLA Ops:
  0.6 3.3 %collective-permute-start.2 = (bf16[8,512,256]{2,1,0:T(8,128)(2,1)}, bf16[8,512,256]{2,1,0:T(8,128)(2,1)S(1)}, u32[]{:S(2)}, u32[]{:S(2)}) collective-permute-start(bf16[8,512,256]{2,1,0:T(8,128)(2,1)} %feet_ref.3), channel_id=1, source_target_pairs={{0,1},{1,0},{2,3},{3,2},{4,5},{5,4},{6,7},{7,6},{8,9},{9,8},{10,11... | collective-permute-start | bytes 6291464 | tf_op jit(solution)/shard_map/ppermute | solution.py:36
  4.4 1.7 %shard_map.86 = (f32[32,256]{1,0:T(8,128)S(1)}, f32[8,128]{1,0:T(8,128)S(1)}, s32[8,128]{1,0:T(8,128)S(1)}, bf16[16,1536]{1,0:T(8,128)(2,1)S(1)}, bf16[16,3072]{...) custom-call(s32[8]{0:T(128)} %bitcast.28, s32[4,8]{1,0:T(4,128)} %bitcast.25, f32[4,8]{1,0:T(4,128)} %bitcast.26, ...), custom_call_target="tpu_custom_call" | custom-call | tf_op jit(solution)/shard_map/pallas_call | solution.py:499
  6.2 1.8 %collective-permute-done.1 = s32[8]{0:T(128)S(1)} collective-permute-done((s32[8]{0:T(128)}, s32[8]{0:T(128)S(1)}, u32[]{:S(2)}, u32[]{:S(2)}) %collective-permute-start.1) | collective-permute-done | bytes 64 | tf_op jit(solution)/shard_map/ppermute | solution.py:36
  8.0 1.3 %shard_map.87 = (bf16[512,128]{1,0:T(8,128)(2,1)}, f32[32,512]{1,0:T(8,128)S(1)}, s32[8,128]{1,0:T(8,128)S(1)}) custom-call(f32[32,256]{1,0:T(8,128)S(1)} %get-tuple-element.25.own_ref, f32[8,4,256]{2,1,0:T(4,128)S(1)} %collective-permute-done.other_ref, f32[8,128]{1,0:T(8,128)S(1)} %get-tuple-element.26.table_ref, ...), custom_call_target="tpu_custom_call" | custom-call | tf_op jit(solution)/shard_map/pallas_call | solution.py:499
  9.3 13.8 %all-to-all-start = ((bf16[128,4,128]{2,1,0:T(4,128)(2,1)}), bf16[128,4,128]{2,1,0:T(4,128)(2,1)S(1)}, u32[]{:S(2)}, u32[]{:S(2)}) async-start(bf16[128,4,128]{2,1,0:T(4,128)(2,1)} %bitcast.4), calls=%async_computation | async-start | bytes 262144 | tf_op jit(solution)/shard_map/all_to_all | solution.py:40
  23.1 3.1 %first_build.1 = (bf16[1536,1536]{1,0:T(8,128)(2,1)}, bf16[256,1536]{1,0:T(8,128)(2,1)}) custom-call(bf16[16,1536]{1,0:T(8,128)(2,1)S(1)} %get-tuple-element.30.left_ref, bf16[16,3072]{1,0:T(8,128)(2,1)S(1)} %get-tuple-element.31.right_ref), custom_call_target="tpu_custom_call" | custom-call | tf_op jit(solution)/shard_map/first_build/pallas_call | solution.py:521
  26.2 8.1 %all-to-all-done = bf16[128,4,128]{2,1,0:T(4,128)(2,1)S(1)} async-done(((bf16[128,4,128]{2,1,0:T(4,128)(2,1)}), bf16[128,4,128]{2,1,0:T(4,128)(2,1)S(1)}, u32[]{:S(2)}, u32[]{:S(2)}) %all-to-all-start) | async-done | bytes 131104 | tf_op jit(solution)/shard_map/all_to_all | solution.py:40
  34.2 1.6 %shard_map.88 = (bf16[512,128]{1,0:T(8,128)(2,1)}, bf16[256,512]{1,0:T(8,128)(2,1)S(1)}) custom-call(bf16[512,128]{1,0:T(8,128)(2,1)S(1)} %bitcast.18, f32[128,128]{1,0:T(8,128)S(1)} %copy-done.1), custom_call_target="tpu_custom_call" | custom-call | tf_op jit(solution)/shard_map/pallas_call | solution.py:499
  35.8 6.2 %all-to-all-start.1 = ((bf16[128,4,128]{2,1,0:T(4,128)(2,1)}), bf16[128,4,128]{2,1,0:T(4,128)(2,1)S(1)}, u32[]{:S(2)}, u32[]{:S(2)}) async-start(bf16[128,4,128]{2,1,0:T(4,128)(2,1)} %bitcast.6), calls=%async_computation.1 | async-start | bytes 262144 | tf_op jit(solution)/shard_map/all_to_all | solution.py:40
  42.0 4.6 %second_build.1.refs_2_ = bf16[1280,1536]{1,0:T(8,128)(2,1)} custom-call(bf16[16,1536]{1,0:T(8,128)(2,1)S(1)} %get-tuple-element.30.left_ref, bf16[16,3072]{1,0:T(8,128)(2,1)S(1)} %get-tuple-element.31.right_ref), custom_call_target="tpu_custom_call" | custom-call | tf_op jit(solution)/shard_map/second_build/pallas_call | solution.py:538
  46.6 6.6 %all-to-all-done.1 = bf16[128,4,128]{2,1,0:T(4,128)(2,1)S(1)} async-done(((bf16[128,4,128]{2,1,0:T(4,128)(2,1)}), bf16[128,4,128]{2,1,0:T(4,128)(2,1)S(1)}, u32[]{:S(2)}, u32[]{:S(2)}) %all-to-all-start.1) | async-done | bytes 131104 | tf_op jit(solution)/shard_map/all_to_all | solution.py:40
  53.2 1.4 %copy-done.2 = bf16[8,512,256]{2,1,0:T(8,128)(2,1)} copy-done((bf16[8,512,256]{2,1,0:T(8,128)(2,1)}, bf16[8,512,256]{2,1,0:T(8,128)(2,1)S(1)}, u32[]{:S(2)}) %copy-start.2) | copy-done | bytes 2097176
  54.6 4.3 %shard_map.89 = (f32[32,512]{1,0:T(8,128)S(1)}, bf16[2,1536,1536]{2,1,0:T(8,128)(2,1)S(1)}, bf16[8,512,256]{2,1,0:T(8,128)(2,1)S(1)}) custom-call(bf16[512,128]{1,0:T(8,128)(2,1)S(1)} %bitcast.16, s32[8,128]{1,0:T(8,128)S(1)} %get-tuple-element.27.tile_rows_ref, s32[8,128]{1,0:T(8,128)S(1)} %get-tuple-element.36.other_rows_ref, ...), custom_call_target="tpu_custom_call" | custom-call | tf_op jit(solution)/shard_map/pallas_call | solution.py:499
  58.8 3.4 %collective-permute-start.3 = (f32[32,512]{1,0:T(8,128)S(1)}, f32[32,512]{1,0:T(8,128)S(1)}, u32[]{:S(2)}, u32[]{:S(2)}) collective-permute-start(f32[32,512]{1,0:T(8,128)S(1)} %get-tuple-element.39.mine_ref), channel_id=1, source_target_pairs={{0,1},{1,0},{2,3},{3,2},{4,5},{5,4},{6,7},{7,6},{8,9},{9,8},{10,11... | collective-permute-start | bytes 196616 | tf_op jit(solution)/shard_map/ppermute | solution.py:36
  62.2 0.9 collective-permute-done.3.theirs_ref
  63.1 1.9 %shard_map.90 = (bf16[512,128]{1,0:T(8,128)(2,1)S(1)}, f32[32,512]{1,0:T(8,128)S(1)}) custom-call(f32[32,512]{1,0:T(8,128)S(1)} %get-tuple-element.39.mine_ref, f32[32,512]{1,0:T(8,128)S(1)} %collective-permute-done.3.theirs_ref, bf16[8,512,256]{2,1,0:T(8,128)(2,1)S(1)} %copy-done, bf16[8,512,256]{2,1,0:T(8,128)(2,1)S(1)} %get-tuple-element.40.other_feet_ref, ...), custom_call_target="tpu_custom_call" | custom-call | tf_op jit(solution)/shard_map/pallas_call | solution.py:499
  65.0 17.0 %all_to_all.25 = bf16[128,4,128]{2,1,0:T(4,128)(2,1)S(1)} all-to-all(bf16[128,4,128]{2,1,0:T(4,128)(2,1)S(1)} %bitcast.22), channel_id=1, replica_groups=mesh['period'=128,'half'=2] {'period'}, dimensions={0} | all-to-all | bytes 262144 | tf_op jit(solution)/shard_map/all_to_all | solution.py:40
  82.8 16.7 %all_to_all.26 = bf16[128,4,128]{2,1,0:T(4,128)(2,1)S(1)} all-to-all(bf16[128,4,128]{2,1,0:T(4,128)(2,1)S(1)} %bitcast.20), channel_id=1, replica_groups=mesh['period'=128,'half'=2] {'period'}, dimensions={0} | all-to-all | bytes 262144 | tf_op jit(solution)/shard_map/all_to_all | solution.py:40
  99.5 1.9 %shard_map.92.mine_ref = f32[32,512]{1,0:T(8,128)S(1)} custom-call(bf16[512,128]{1,0:T(8,128)(2,1)S(1)} %bitcast.17, s32[8,128]{1,0:T(8,128)S(1)} %get-tuple-element.27.tile_rows_ref, s32[8,128]{1,0:T(8,128)S(1)} %get-tuple-element.36.other_rows_ref, bf16[2,1536,1536]{2,1,0:T(8,128)(2,1)S(1)} %get-tuple-element.43.refs_0_), custom_call_target="tpu_custom_call" | custom-call | tf_op jit(solution)/shard_map/pallas_call | solution.py:499
  101.4 3.2 %collective-permute-start.4 = (f32[32,512]{1,0:T(8,128)S(1)}, f32[32,512]{1,0:T(8,128)S(1)}, u32[]{:S(2)}, u32[]{:S(2)}) collective-permute-start(f32[32,512]{1,0:T(8,128)S(1)} %shard_map.92.mine_ref), channel_id=1, source_target_pairs={{0,1},{1,0},{2,3},{3,2},{4,5},{5,4},{6,7},{7,6},{8,9},{9,8},{10,11... | collective-permute-start | bytes 196616 | tf_op jit(solution)/shard_map/ppermute | solution.py:36
  104.7 0.9 collective-permute-done.4.theirs_ref
  105.6 1.5 %shard_map.93 = (f32[128,128]{1,0:T(8,128)S(1)}, f32[32,512]{1,0:T(8,128)S(1)}) custom-call(f32[32,512]{1,0:T(8,128)S(1)} %shard_map.92.mine_ref, f32[32,512]{1,0:T(8,128)S(1)} %collective-permute-done.4.theirs_ref, bf16[8,512,256]{2,1,0:T(8,128)(2,1)S(1)} %copy-done, bf16[8,512,256]{2,1,0:T(8,128)(2,1)S(1)} %get-tuple-element.40.other_feet_ref, ...), custom_call_target="tpu_custom_call" | custom-call | tf_op jit(solution)/shard_map/pallas_call | solution.py:499
  107.0 16.3 %all_to_all.27 = f32[128,1,128]{2,1,0:T(1,128)S(1)} all-to-all(f32[128,1,128]{2,1,0:T(1,128)S(1)} %bitcast.23), channel_id=1, replica_groups=mesh['period'=128,'half'=2] {'period'}, dimensions={0} | all-to-all | bytes 131072 | tf_op jit(solution)/shard_map/all_to_all | solution.py:40
  123.3 0.9 finish.1
  (10 shorter events, 1.3 us)
Async XLA Ops:
  0.6 52.6 %collective-permute-start.2 = (bf16[8,512,256]{2,1,0:T(8,128)(2,1)}, bf16[8,512,256]{2,1,0:T(8,128)(2,1)S(1)}, u32[]{:S(2)}, u32[]{:S(2)}) collective-permute-start(bf16[8,512,256]{2,1,0:T(8,128)(2,1)} %feet_ref.3), channel_id=1, source_target_pairs={{0,1},{1,0},{2,3},{3,2},{4,5},{5,4},{6,7},{7,6},{8,9},{9,8},{10,11... | collective-permute-start | bytes 6291464 | tf_op jit(solution)/shard_map/ppermute | solution.py:36
  3.9 4.0 %collective-permute-start = (f32[8,4,256]{2,1,0:T(4,128)}, f32[8,4,256]{2,1,0:T(4,128)S(1)}, u32[]{:S(2)}, u32[]{:S(2)}) collective-permute-start(f32[8,4,256]{2,1,0:T(4,128)} %own_in.1), channel_id=1, source_target_pairs={{0,1},{1,0},{2,3},{3,2},{4,5},{5,4},{6,7},{7,6},{8,9},{9,8},{10,11... | collective-permute-start | bytes 98312 | tf_op jit(solution)/shard_map/ppermute | solution.py:36
  4.0 3.9 %collective-permute-start.1 = (s32[8]{0:T(128)}, s32[8]{0:T(128)S(1)}, u32[]{:S(2)}, u32[]{:S(2)}) collective-permute-start(s32[8]{0:T(128)} %bitcast.27), channel_id=1, source_target_pairs={{0,1},{1,0},{2,3},{3,2},{4,5},{5,4},{6,7},{7,6},{8,9},{9,8},{10,11... | collective-permute-start | bytes 104 | tf_op jit(solution)/shard_map/ppermute | solution.py:36
  4.4 29.8 %copy-start.1 = (f32[128,128]{1,0:T(8,128)S(1)}, f32[128,128]{1,0:T(8,128)}, u32[]{:S(2)}) copy-start(f32[128,128]{1,0:T(8,128)} %temporal_ref.3) | copy-start | bytes 196612
  9.3 25.0 %all-to-all-start = ((bf16[128,4,128]{2,1,0:T(4,128)(2,1)}), bf16[128,4,128]{2,1,0:T(4,128)(2,1)S(1)}, u32[]{:S(2)}, u32[]{:S(2)}) async-start(bf16[128,4,128]{2,1,0:T(4,128)(2,1)} %bitcast.4), calls=%async_computation | async-start | bytes 262144 | tf_op jit(solution)/shard_map/all_to_all | solution.py:40
  35.8 17.4 %all-to-all-start.1 = ((bf16[128,4,128]{2,1,0:T(4,128)(2,1)}), bf16[128,4,128]{2,1,0:T(4,128)(2,1)S(1)}, u32[]{:S(2)}, u32[]{:S(2)}) async-start(bf16[128,4,128]{2,1,0:T(4,128)(2,1)} %bitcast.6), calls=%async_computation.1 | async-start | bytes 262144 | tf_op jit(solution)/shard_map/all_to_all | solution.py:40
  53.2 1.4 %copy-start.2 = (bf16[8,512,256]{2,1,0:T(8,128)(2,1)}, bf16[8,512,256]{2,1,0:T(8,128)(2,1)S(1)}, u32[]{:S(2)}) copy-start(bf16[8,512,256]{2,1,0:T(8,128)(2,1)S(1)} %collective-permute-done.2.refs_3_) | copy-start | bytes 6291460
  54.6 8.6 %copy-start = (bf16[8,512,256]{2,1,0:T(8,128)(2,1)S(1)}, bf16[8,512,256]{2,1,0:T(8,128)(2,1)}, u32[]{:S(2)}) copy-start(bf16[8,512,256]{2,1,0:T(8,128)(2,1)} %feet_ref.3) | copy-start | bytes 6291460
  58.8 4.3 %collective-permute-start.3 = (f32[32,512]{1,0:T(8,128)S(1)}, f32[32,512]{1,0:T(8,128)S(1)}, u32[]{:S(2)}, u32[]{:S(2)}) collective-permute-start(f32[32,512]{1,0:T(8,128)S(1)} %get-tuple-element.39.mine_ref), channel_id=1, source_target_pairs={{0,1},{1,0},{2,3},{3,2},{4,5},{5,4},{6,7},{7,6},{8,9},{9,8},{10,11... | collective-permute-start | bytes 196616 | tf_op jit(solution)/shard_map/ppermute | solution.py:36
  101.4 4.1 %collective-permute-start.4 = (f32[32,512]{1,0:T(8,128)S(1)}, f32[32,512]{1,0:T(8,128)S(1)}, u32[]{:S(2)}, u32[]{:S(2)}) collective-permute-start(f32[32,512]{1,0:T(8,128)S(1)} %shard_map.92.mine_ref), channel_id=1, source_target_pairs={{0,1},{1,0},{2,3},{3,2},{4,5},{5,4},{6,7},{7,6},{8,9},{9,8},{10,11... | collective-permute-start | bytes 196616 | tf_op jit(solution)/shard_map/ppermute | solution.py:36

commit v2 on v1

--- a/solution.py
+++ b/solution.py
@@ -194,7 +194,7 @@
     copies[5].wait()
 
 
-def start_kernel(own_ref, other_ref, table_ref, tile_rows_ref, feet_ref, others_ref, out_ref, probes_ref, other_rows_ref):
+def start_kernel(own_ref, other_ref, table_ref, tile_rows_ref, feet_ref, out_ref, probes_ref):
     half = lax.axis_index("half")
     block_count, probe_count, half_sound = other_ref.shape
     own_at = pl.multiple_of(half * half_sound, LANES)
@@ -203,13 +203,6 @@
     for probe in range(probe_count):
         rows = slice(probe * block_count, (probe + 1) * block_count)
         probes_ref[rows, pl.ds(other_at, half_sound)] = other_ref[:, probe, :]
-    square = (block_count, block_count)
-    on_diagonal = lax.broadcasted_iota(jnp.int32, square, 0) == lax.broadcasted_iota(
-        jnp.int32, square, 1
-    )
-    others = jnp.where(on_diagonal, jnp.broadcast_to(others_ref[...], square), 0)
-    others = jnp.sum(others, axis=1, keepdims=True)
-    other_rows_ref[...] = jnp.broadcast_to(others, other_rows_ref.shape)
     pieces = adjoint_pieces(probes_ref[...].astype(jnp.bfloat16), feet_ref)
     table, tile_rows = table_ref[...], tile_rows_ref[...]
     _, lane = tile_iotas()
@@ -259,8 +252,23 @@
         copy.wait()
 
 
-def second_build_kernel(left_ref, right_ref, out_ref):
-    out_ref[...] = spatial_values(left_ref[...], right_ref[...])
+def second_build_kernel(left_ref, right_ref, out, buffers, sems):
+    half_cells = left_ref.shape[1]
+    count, depth = buffers.shape[:2]
+    copies = []
+    for place in range(count):
+        at = depth * (place + 1)
+        buffers[place] = spatial_values(
+            left_ref[:, at : at + depth], right_ref[:, half_cells:]
+        )
+        copies.append(
+            pltpu.make_async_copy(
+                buffers.at[place], out.at[at - depth : at], sems.at[place]
+            )
+        )
+        copies[-1].start()
+    for copy in copies:
+        copy.wait()
 
 
 def mix(received, choice, temporal):
@@ -278,7 +286,15 @@
     return dot(jnp.concatenate([upper, lower], axis=0), choice).T.astype(jnp.bfloat16)
 
 
-def first_mix_kernel(top_count, received_ref, temporal_ref, out_ref, choice_ref):
+def first_mix_kernel(top_count, received_ref, temporal_ref, others_ref, out_ref, choice_ref, other_rows_ref):
+    block_count = others_ref.shape[1]
+    square = (block_count, block_count)
+    on_diagonal = lax.broadcasted_iota(jnp.int32, square, 0) == lax.broadcasted_iota(
+        jnp.int32, square, 1
+    )
+    others = jnp.where(on_diagonal, jnp.broadcast_to(others_ref[...], square), 0)
+    others = jnp.sum(others, axis=1, keepdims=True)
+    other_rows_ref[...] = jnp.broadcast_to(others, other_rows_ref.shape)
     periods = temporal_ref.shape[0]
     wide = received_ref[...].astype(jnp.float32).T
     shape = (periods, wide.shape[1])
@@ -538,12 +554,12 @@
         return pl.pallas_call(
             second_build_kernel,
             out_shape=pltpu.HBM((half_cells - depth, half_cells), bf16),
-            grid=(block_rows - 1,),
-            in_specs=[
-                pl.BlockSpec((16, depth), lambda i: (0, i + 1)),
-                pl.BlockSpec((16, half_cells), lambda i: (0, 1)),
+            in_specs=[vmem, vmem],
+            out_specs=hbm,
+            scratch_shapes=[
+                pltpu.VMEM((block_rows - 1, depth, half_cells), bf16),
+                pltpu.SemaphoreType.DMA((block_rows - 1,)),
             ],
-            out_specs=pl.BlockSpec((depth, half_cells), lambda i: (i, 0)),
             compiler_params=small,
             name="second_build",
         )(in_vmem(left), in_vmem(right))
@@ -575,7 +591,6 @@
 
     tiles = window_tiles.reshape(-1)
     other_probes = from_other_half(probes)
-    other_tiles = from_other_half(tiles)
     own_probes, table, tile_rows, left, right, first_feet = call(
         prepare_kernel,
         (),
@@ -598,23 +613,25 @@
         ),
         (tiles, owners.T, lag_weights.T, probes, coords, footprints),
     )
-    to_mix, all_probes, other_rows = call(
-        start_kernel,
-        (),
-        (own_probes, other_probes, table, tile_rows, first_feet, other_tiles.reshape(1, -1)),
-        (wire, vectors, pltpu.VMEM((block_count, LANES), jnp.int32)),
+    to_mix, all_probes = call(
+        start_kernel, (), (own_probes, other_probes, table, tile_rows, first_feet), (wire, vectors)
     )
     received = send(to_mix)
     other_feet = from_other_half(footprints)
+    other_tiles = from_other_half(tiles)
     own_spatial, top_spatial = first_build()
     received, own_spatial, top_spatial = lax.optimization_barrier(
         (received, own_spatial, top_spatial)
     )
-    mixed, choice = call(
+    mixed, choice, other_rows = call(
         functools.partial(first_mix_kernel, top_count),
         (),
-        (received, temporal),
-        (wire, pltpu.VMEM((2 * periods, periods * HALF_SUBLANES), bf16)),
+        (received, temporal, other_tiles.reshape(1, -1)),
+        (
+            wire,
+            pltpu.VMEM((2 * periods, periods * HALF_SUBLANES), bf16),
+            pltpu.VMEM((block_count, LANES), jnp.int32),
+        ),
     )
     rest_spatial = second_build()
     mine, theirs, kept, other_feet = spatial_step(send(mixed), None)

time: 125 us -> 124 us (level)
  Pallas kernels: 23.4 us -> 22.1 us
    pallas_call x1, Pallas kernels: 4.64 us -> 3.31 us  [second_build(): pl.pallas_call(second_build_kernel, out_shape=pltpu.HBM((half_cells - dep...]
  transfers between devices with their start and end apart: 7 -> 7, of which waited for: 5 -> 5; matrix products, arithmetic and copies ran while one was open for 0% -> 0% of each run, Pallas kernels for 10% -> 9%
where the time goes in v2:
time: 124 us
  blocking collectives  50.1 us (40%)
  starting transfers between devices  30.6 us (25%)
  Pallas kernels  22.1 us (18%)
  waiting for transfers between devices  19.1 us (15%)
  local copies, waits for them, and re-layouts  1.38 us (1%)
    all_to_all x3, blocking collectives, exchange(): lax.all_to_all(value, 'period', split_axis=0, concat_axis=0, tiled=True)  50.1 us
    all_to_all x2, starting transfers between devices, exchange(): lax.all_to_all(value, 'period', split_axis=0, concat_axis=0, tiled=True)  20.1 us
    all_to_all x2, waiting for transfers between devices, exchange(): lax.all_to_all(value, 'period', split_axis=0, concat_axis=0, tiled=True)  15.1 us
    pallas_call x8, Pallas kernels, call(): pl.pallas_call(kernel, out_shape=outputs, in_specs=[smem] * len(scalars)...  14.8 us
    ppermute x5, starting transfers between devices, from_other_half(): return lax.ppermute(value, 'half', [(0, 1), (1, 0)])  10.4 us
    ppermute x5, waiting for transfers between devices, from_other_half(): return lax.ppermute(value, 'half', [(0, 1), (1, 0)])  4.02 us
    pallas_call x1, Pallas kernels, second_build(): pl.pallas_call(second_build_kernel, out_shape=pltpu.HBM((half_cells - dep...  3.31 us
    pallas_call x1, Pallas kernels, first_build(): pl.pallas_call(first_build_kernel, out_shape=(pltpu.HBM((half_cells, half...  3.06 us
  transfers between devices with their start and end apart: 7, of which 5 were waited for; matrix products, arithmetic and copies ran while one was open for 0% of the time, Pallas kernels for 9%

profile of v2, /device:TPU:1, one launch (start us, length us, event | category | flops | bytes accessed | tf_op | source)
XLA Modules:
  0.0 124.0 jit_solution(331432335716150730)
XLA Ops:
  0.6 3.3 %collective-permute-start.2 = (bf16[8,512,256]{2,1,0:T(8,128)(2,1)}, bf16[8,512,256]{2,1,0:T(8,128)(2,1)S(1)}, u32[]{:S(2)}, u32[]{:S(2)}) collective-permute-start(bf16[8,512,256]{2,1,0:T(8,128)(2,1)} %feet_ref.3), channel_id=1, source_target_pairs={{0,1},{1,0},{2,3},{3,2},{4,5},{5,4},{6,7},{7,6},{8,9},{9,8},{10,11... | collective-permute-start | bytes 6291464 | tf_op jit(solution)/shard_map/ppermute | solution.py:36
  4.0 1.7 %shard_map.86 = (f32[32,256]{1,0:T(8,128)S(1)}, f32[8,128]{1,0:T(8,128)S(1)}, s32[8,128]{1,0:T(8,128)S(1)}, bf16[16,1536]{1,0:T(8,128)(2,1)S(1)}, bf16[16,3072]{...) custom-call(s32[8]{0:T(128)} %bitcast.27, s32[4,8]{1,0:T(4,128)} %bitcast.25, f32[4,8]{1,0:T(4,128)} %bitcast.26, ...), custom_call_target="tpu_custom_call" | custom-call | tf_op jit(solution)/shard_map/pallas_call | solution.py:515
  5.7 2.2 %collective-permute-done.other_ref = f32[8,4,256]{2,1,0:T(4,128)S(1)} collective-permute-done((f32[8,4,256]{2,1,0:T(4,128)}, f32[8,4,256]{2,1,0:T(4,128)S(1)}, u32[]{:S(2)}, u32[]{:S(2)}) %collective-permute-start) | collective-permute-done | bytes 32800 | tf_op jit(solution)/shard_map/ppermute | solution.py:36
  8.0 1.3 %shard_map.87 = (bf16[512,128]{1,0:T(8,128)(2,1)}, f32[32,512]{1,0:T(8,128)S(1)}) custom-call(f32[32,256]{1,0:T(8,128)S(1)} %get-tuple-element.25.own_ref, f32[8,4,256]{2,1,0:T(4,128)S(1)} %collective-permute-done.other_ref, f32[8,128]{1,0:T(8,128)S(1)} %get-tuple-element.26.table_ref, s32[8,128]{1,0:T(8,128)S(1)} %get-tuple-element.27.tile_rows_ref, ...), custom_call_target="tpu_custom_call" | custom-call | tf_op jit(solution)/shard_map/pallas_call | solution.py:515
  9.3 13.8 %all-to-all-start = ((bf16[128,4,128]{2,1,0:T(4,128)(2,1)}), bf16[128,4,128]{2,1,0:T(4,128)(2,1)S(1)}, u32[]{:S(2)}, u32[]{:S(2)}) async-start(bf16[128,4,128]{2,1,0:T(4,128)(2,1)} %bitcast.3), calls=%async_computation | async-start | bytes 262144 | tf_op jit(solution)/shard_map/all_to_all | solution.py:40
  23.8 3.1 %first_build.1 = (bf16[1536,1536]{1,0:T(8,128)(2,1)}, bf16[256,1536]{1,0:T(8,128)(2,1)}) custom-call(bf16[16,1536]{1,0:T(8,128)(2,1)S(1)} %get-tuple-element.30.left_ref, bf16[16,3072]{1,0:T(8,128)(2,1)S(1)} %get-tuple-element.31.right_ref), custom_call_target="tpu_custom_call" | custom-call | tf_op jit(solution)/shard_map/first_build/pallas_call | solution.py:537
  26.9 7.3 %all-to-all-done = bf16[128,4,128]{2,1,0:T(4,128)(2,1)S(1)} async-done(((bf16[128,4,128]{2,1,0:T(4,128)(2,1)}), bf16[128,4,128]{2,1,0:T(4,128)(2,1)S(1)}, u32[]{:S(2)}, u32[]{:S(2)}) %all-to-all-start) | async-done | bytes 131104 | tf_op jit(solution)/shard_map/all_to_all | solution.py:40
  34.2 1.6 %shard_map.88 = (bf16[512,128]{1,0:T(8,128)(2,1)}, bf16[256,512]{1,0:T(8,128)(2,1)S(1)}, s32[8,128]{1,0:T(8,128)S(1)}) custom-call(bf16[512,128]{1,0:T(8,128)(2,1)S(1)} %bitcast.18, f32[128,128]{1,0:T(8,128)S(1)} %copy-done.1, s32[1,8]{1,0:T(1,128)S(1)} %bitcast.24), custom_call_target="tpu_custom_call" | custom-call | tf_op jit(solution)/shard_map/pallas_call | solution.py:515
  35.8 6.3 %all-to-all-start.1 = ((bf16[128,4,128]{2,1,0:T(4,128)(2,1)}), bf16[128,4,128]{2,1,0:T(4,128)(2,1)S(1)}, u32[]{:S(2)}, u32[]{:S(2)}) async-start(bf16[128,4,128]{2,1,0:T(4,128)(2,1)} %bitcast.6), calls=%async_computation.1 | async-start | bytes 262144 | tf_op jit(solution)/shard_map/all_to_all | solution.py:40
  42.1 3.3 %second_build.1.refs_2_ = bf16[1280,1536]{1,0:T(8,128)(2,1)} custom-call(bf16[16,1536]{1,0:T(8,128)(2,1)S(1)} %get-tuple-element.30.left_ref, bf16[16,3072]{1,0:T(8,128)(2,1)S(1)} %get-tuple-element.31.right_ref), custom_call_target="tpu_custom_call" | custom-call | tf_op jit(solution)/shard_map/second_build/pallas_call | solution.py:554
  45.5 7.8 %all-to-all-done.1 = bf16[128,4,128]{2,1,0:T(4,128)(2,1)S(1)} async-done(((bf16[128,4,128]{2,1,0:T(4,128)(2,1)}), bf16[128,4,128]{2,1,0:T(4,128)(2,1)S(1)}, u32[]{:S(2)}, u32[]{:S(2)}) %all-to-all-start.1) | async-done | bytes 131104 | tf_op jit(solution)/shard_map/all_to_all | solution.py:40
  53.2 1.4 %copy-done.2 = bf16[8,512,256]{2,1,0:T(8,128)(2,1)} copy-done((bf16[8,512,256]{2,1,0:T(8,128)(2,1)}, bf16[8,512,256]{2,1,0:T(8,128)(2,1)S(1)}, u32[]{:S(2)}) %copy-start.2) | copy-done | bytes 2097176
  54.6 4.3 %shard_map.89 = (f32[32,512]{1,0:T(8,128)S(1)}, bf16[2,1536,1536]{2,1,0:T(8,128)(2,1)S(1)}, bf16[8,512,256]{2,1,0:T(8,128)(2,1)S(1)}) custom-call(bf16[512,128]{1,0:T(8,128)(2,1)S(1)} %bitcast.16, s32[8,128]{1,0:T(8,128)S(1)} %get-tuple-element.27.tile_rows_ref, s32[8,128]{1,0:T(8,128)S(1)} %get-tuple-element.36.other_rows_ref, ...), custom_call_target="tpu_custom_call" | custom-call | tf_op jit(solution)/shard_map/pallas_call | solution.py:515
  58.9 3.3 %collective-permute-start.3 = (f32[32,512]{1,0:T(8,128)S(1)}, f32[32,512]{1,0:T(8,128)S(1)}, u32[]{:S(2)}, u32[]{:S(2)}) collective-permute-start(f32[32,512]{1,0:T(8,128)S(1)} %get-tuple-element.39.mine_ref), channel_id=1, source_target_pairs={{0,1},{1,0},{2,3},{3,2},{4,5},{5,4},{6,7},{7,6},{8,9},{9,8},{10,11... | collective-permute-start | bytes 196616 | tf_op jit(solution)/shard_map/ppermute | solution.py:36
  62.2 0.9 collective-permute-done.3.theirs_ref
  63.1 1.9 %shard_map.90 = (bf16[512,128]{1,0:T(8,128)(2,1)S(1)}, f32[32,512]{1,0:T(8,128)S(1)}) custom-call(f32[32,512]{1,0:T(8,128)S(1)} %get-tuple-element.39.mine_ref, f32[32,512]{1,0:T(8,128)S(1)} %collective-permute-done.3.theirs_ref, bf16[8,512,256]{2,1,0:T(8,128)(2,1)S(1)} %copy-done, bf16[8,512,256]{2,1,0:T(8,128)(2,1)S(1)} %get-tuple-element.40.other_feet_ref, ...), custom_call_target="tpu_custom_call" | custom-call | tf_op jit(solution)/shard_map/pallas_call | solution.py:515
  65.0 17.1 %all_to_all.25 = bf16[128,4,128]{2,1,0:T(4,128)(2,1)S(1)} all-to-all(bf16[128,4,128]{2,1,0:T(4,128)(2,1)S(1)} %bitcast.22), channel_id=1, replica_groups=mesh['period'=128,'half'=2] {'period'}, dimensions={0} | all-to-all | bytes 262144 | tf_op jit(solution)/shard_map/all_to_all | solution.py:40
  82.8 16.8 %all_to_all.26 = bf16[128,4,128]{2,1,0:T(4,128)(2,1)S(1)} all-to-all(bf16[128,4,128]{2,1,0:T(4,128)(2,1)S(1)} %bitcast.20), channel_id=1, replica_groups=mesh['period'=128,'half'=2] {'period'}, dimensions={0} | all-to-all | bytes 262144 | tf_op jit(solution)/shard_map/all_to_all | solution.py:40
  99.6 1.9 %shard_map.92.mine_ref = f32[32,512]{1,0:T(8,128)S(1)} custom-call(bf16[512,128]{1,0:T(8,128)(2,1)S(1)} %bitcast.17, s32[8,128]{1,0:T(8,128)S(1)} %get-tuple-element.27.tile_rows_ref, s32[8,128]{1,0:T(8,128)S(1)} %get-tuple-element.36.other_rows_ref, bf16[2,1536,1536]{2,1,0:T(8,128)(2,1)S(1)} %get-tuple-element.43.refs_0_), custom_call_target="tpu_custom_call" | custom-call | tf_op jit(solution)/shard_map/pallas_call | solution.py:515
  101.5 3.0 %collective-permute-start.4 = (f32[32,512]{1,0:T(8,128)S(1)}, f32[32,512]{1,0:T(8,128)S(1)}, u32[]{:S(2)}, u32[]{:S(2)}) collective-permute-start(f32[32,512]{1,0:T(8,128)S(1)} %shard_map.92.mine_ref), channel_id=1, source_target_pairs={{0,1},{1,0},{2,3},{3,2},{4,5},{5,4},{6,7},{7,6},{8,9},{9,8},{10,11... | collective-permute-start | bytes 196616 | tf_op jit(solution)/shard_map/ppermute | solution.py:36
  104.4 0.9 collective-permute-done.4.theirs_ref
  105.3 1.5 %shard_map.93 = (f32[128,128]{1,0:T(8,128)S(1)}, f32[32,512]{1,0:T(8,128)S(1)}) custom-call(f32[32,512]{1,0:T(8,128)S(1)} %shard_map.92.mine_ref, f32[32,512]{1,0:T(8,128)S(1)} %collective-permute-done.4.theirs_ref, bf16[8,512,256]{2,1,0:T(8,128)(2,1)S(1)} %copy-done, bf16[8,512,256]{2,1,0:T(8,128)(2,1)S(1)} %get-tuple-element.40.other_feet_ref, ...), custom_call_target="tpu_custom_call" | custom-call | tf_op jit(solution)/shard_map/pallas_call | solution.py:515
  106.8 16.3 %all_to_all.27 = f32[128,1,128]{2,1,0:T(1,128)S(1)} all-to-all(f32[128,1,128]{2,1,0:T(1,128)S(1)} %bitcast.23), channel_id=1, replica_groups=mesh['period'=128,'half'=2] {'period'}, dimensions={0} | all-to-all | bytes 131072 | tf_op jit(solution)/shard_map/all_to_all | solution.py:40
  123.1 0.9 finish.1
  (12 shorter events, 1.6 us)
Async XLA Ops:
  0.6 52.6 %collective-permute-start.2 = (bf16[8,512,256]{2,1,0:T(8,128)(2,1)}, bf16[8,512,256]{2,1,0:T(8,128)(2,1)S(1)}, u32[]{:S(2)}, u32[]{:S(2)}) collective-permute-start(bf16[8,512,256]{2,1,0:T(8,128)(2,1)} %feet_ref.3), channel_id=1, source_target_pairs={{0,1},{1,0},{2,3},{3,2},{4,5},{5,4},{6,7},{7,6},{8,9},{9,8},{10,11... | collective-permute-start | bytes 6291464 | tf_op jit(solution)/shard_map/ppermute | solution.py:36
  3.9 4.0 %collective-permute-start = (f32[8,4,256]{2,1,0:T(4,128)}, f32[8,4,256]{2,1,0:T(4,128)S(1)}, u32[]{:S(2)}, u32[]{:S(2)}) collective-permute-start(f32[8,4,256]{2,1,0:T(4,128)} %own_in.1), channel_id=1, source_target_pairs={{0,1},{1,0},{2,3},{3,2},{4,5},{5,4},{6,7},{7,6},{8,9},{9,8},{10,11... | collective-permute-start | bytes 98312 | tf_op jit(solution)/shard_map/ppermute | solution.py:36
  4.0 19.0 %copy-start.3 = (s32[8,1]{0,1:T(1,128)S(1)}, s32[8,1]{0,1:T(1,128)}, u32[]{:S(2)}) copy-start(s32[8,1]{0,1:T(1,128)} %param.11) | copy-start | bytes 100
  4.0 30.2 %copy-start.1 = (f32[128,128]{1,0:T(8,128)S(1)}, f32[128,128]{1,0:T(8,128)}, u32[]{:S(2)}) copy-start(f32[128,128]{1,0:T(8,128)} %temporal_ref.3) | copy-start | bytes 196612
  9.3 25.0 %all-to-all-start = ((bf16[128,4,128]{2,1,0:T(4,128)(2,1)}), bf16[128,4,128]{2,1,0:T(4,128)(2,1)S(1)}, u32[]{:S(2)}, u32[]{:S(2)}) async-start(bf16[128,4,128]{2,1,0:T(4,128)(2,1)} %bitcast.3), calls=%async_computation | async-start | bytes 262144 | tf_op jit(solution)/shard_map/all_to_all | solution.py:40
  23.1 11.1 %collective-permute-start.1 = (s32[8]{0:T(128)S(1)}, s32[8]{0:T(128)S(1)}, u32[]{:S(2)}, u32[]{:S(2)}) collective-permute-start(s32[8]{0:T(128)S(1)} %bitcast.28), channel_id=1, source_target_pairs={{0,1},{1,0},{2,3},{3,2},{4,5},{5,4},{6,7},{7,6},{8,9},{9,8},{10,11... | collective-permute-start | bytes 104 | tf_op jit(solution)/shard_map/ppermute | solution.py:36
  35.8 17.4 %all-to-all-start.1 = ((bf16[128,4,128]{2,1,0:T(4,128)(2,1)}), bf16[128,4,128]{2,1,0:T(4,128)(2,1)S(1)}, u32[]{:S(2)}, u32[]{:S(2)}) async-start(bf16[128,4,128]{2,1,0:T(4,128)(2,1)} %bitcast.6), calls=%async_computation.1 | async-start | bytes 262144 | tf_op jit(solution)/shard_map/all_to_all | solution.py:40
  53.2 1.4 %copy-start.2 = (bf16[8,512,256]{2,1,0:T(8,128)(2,1)}, bf16[8,512,256]{2,1,0:T(8,128)(2,1)S(1)}, u32[]{:S(2)}) copy-start(bf16[8,512,256]{2,1,0:T(8,128)(2,1)S(1)} %collective-permute-done.2.refs_3_) | copy-start | bytes 6291460
  54.6 8.5 %copy-start = (bf16[8,512,256]{2,1,0:T(8,128)(2,1)S(1)}, bf16[8,512,256]{2,1,0:T(8,128)(2,1)}, u32[]{:S(2)}) copy-start(bf16[8,512,256]{2,1,0:T(8,128)(2,1)} %feet_ref.3) | copy-start | bytes 6291460
  58.9 4.2 %collective-permute-start.3 = (f32[32,512]{1,0:T(8,128)S(1)}, f32[32,512]{1,0:T(8,128)S(1)}, u32[]{:S(2)}, u32[]{:S(2)}) collective-permute-start(f32[32,512]{1,0:T(8,128)S(1)} %get-tuple-element.39.mine_ref), channel_id=1, source_target_pairs={{0,1},{1,0},{2,3},{3,2},{4,5},{5,4},{6,7},{7,6},{8,9},{9,8},{10,11... | collective-permute-start | bytes 196616 | tf_op jit(solution)/shard_map/ppermute | solution.py:36
  101.5 3.9 %collective-permute-start.4 = (f32[32,512]{1,0:T(8,128)S(1)}, f32[32,512]{1,0:T(8,128)S(1)}, u32[]{:S(2)}, u32[]{:S(2)}) collective-permute-start(f32[32,512]{1,0:T(8,128)S(1)} %shard_map.92.mine_ref), channel_id=1, source_target_pairs={{0,1},{1,0},{2,3},{3,2},{4,5},{5,4},{6,7},{7,6},{8,9},{9,8},{10,11... | collective-permute-start | bytes 196616 | tf_op jit(solution)/shard_map/ppermute | solution.py:36

commit v3 on v2

--- a/solution.py
+++ b/solution.py
@@ -313,6 +313,11 @@
     out_ref[...] = mix(received_ref[...], choice_ref[...], temporal_ref[...])
 
 
+def column_spans(count, width):
+    ends = [0, width + width // 4, 2 * width + width // 2, count]
+    return list(zip(ends[:-1], ends[1:]))
+
+
 def spatial_kernel(block_count, depth, width, streamed, received_ref, tile_rows_ref, other_rows_ref, *refs):
     if streamed:
         own_in, top_in, rest_in, feet_in, out_ref, kept_ref, feet_ref, field, total, sems = refs
@@ -327,8 +332,8 @@
             (own_in.at[at : at + depth, at:], kept_ref.at[0, at : at + depth, at:])
             for at in range(0, half_cells, depth)
         ]
-        for at in range(0, half_cells, width):
-            columns = slice(at, at + width)
+        for at, end in column_spans(half_cells, width):
+            columns = slice(at, end)
             pairs.append((top_in.at[:, columns], kept_ref.at[1, :depth, columns]))
             pairs.append((rest_in.at[:, columns], kept_ref.at[1, depth:, columns]))
         pairs.append((feet_in, feet_ref))
@@ -373,11 +378,10 @@
         if end < half_cells:
             value = value + dot(cells[:, end:], kept_ref[0, at:end, end:], ((1,), (1,)))
         total[:, at:end] = value
-    for place, at in enumerate(range(0, half_cells, width)):
+    for place, (at, end) in enumerate(column_spans(half_cells, width)):
         for copy in other_copies[2 * place : 2 * place + 2]:
             copy.wait()
-        start = half_cells + at
-        total[:, start : start + width] = dot(cells, kept_ref[1, :, at : at + width])
+        total[:, half_cells + at : half_cells + end] = dot(cells, kept_ref[1, :, at:end])
     nothing = jnp.zeros((block_count, LANES), jnp.float32)
     for side, rows_ref in enumerate((tile_rows_ref, other_rows_ref)):
         first_tile = rows_ref[...]

time: 124 us -> 124 us (level)
  no operation moved by 1% of the time
where the time goes in v3:
time: 124 us
  blocking collectives  50.1 us (40%)
  starting transfers between devices  30.6 us (25%)
  Pallas kernels  22 us (18%)
  waiting for transfers between devices  19.1 us (15%)
  local copies, waits for them, and re-layouts  1.38 us (1%)
    all_to_all x3, blocking collectives, exchange(): lax.all_to_all(value, 'period', split_axis=0, concat_axis=0, tiled=True)  50.1 us
    all_to_all x2, starting transfers between devices, exchange(): lax.all_to_all(value, 'period', split_axis=0, concat_axis=0, tiled=True)  20.1 us
    all_to_all x2, waiting for transfers between devices, exchange(): lax.all_to_all(value, 'period', split_axis=0, concat_axis=0, tiled=True)  15.1 us
    pallas_call x8, Pallas kernels, call(): pl.pallas_call(kernel, out_shape=outputs, in_specs=[smem] * len(scalars)...  14.8 us
    ppermute x5, starting transfers between devices, from_other_half(): return lax.ppermute(value, 'half', [(0, 1), (1, 0)])  10.5 us
    ppermute x5, waiting for transfers between devices, from_other_half(): return lax.ppermute(value, 'half', [(0, 1), (1, 0)])  4.02 us
    pallas_call x1, Pallas kernels, second_build(): pl.pallas_call(second_build_kernel, out_shape=pltpu.HBM((half_cells - dep...  3.31 us
    pallas_call x1, Pallas kernels, first_build(): pl.pallas_call(first_build_kernel, out_shape=(pltpu.HBM((half_cells, half...  3.06 us
  transfers between devices with their start and end apart: 7, of which 5 were waited for; matrix products, arithmetic and copies ran while one was open for 0% of the time, Pallas kernels for 9%

profile of v3, /device:TPU:1, one launch (start us, length us, event | category | flops | bytes accessed | tf_op | source)
XLA Modules:
  0.0 123.9 jit_solution(5017300442891445093)
XLA Ops:
  0.6 3.3 %collective-permute-start.2 = (bf16[8,512,256]{2,1,0:T(8,128)(2,1)}, bf16[8,512,256]{2,1,0:T(8,128)(2,1)S(1)}, u32[]{:S(2)}, u32[]{:S(2)}) collective-permute-start(bf16[8,512,256]{2,1,0:T(8,128)(2,1)} %feet_ref.3), channel_id=1, source_target_pairs={{0,1},{1,0},{2,3},{3,2},{4,5},{5,4},{6,7},{7,6},{8,9},{9,8},{10,11... | collective-permute-start | bytes 6291464 | tf_op jit(solution)/shard_map/ppermute | solution.py:36
  4.0 1.7 %shard_map.86 = (f32[32,256]{1,0:T(8,128)S(1)}, f32[8,128]{1,0:T(8,128)S(1)}, s32[8,128]{1,0:T(8,128)S(1)}, bf16[16,1536]{1,0:T(8,128)(2,1)S(1)}, bf16[16,3072]{...) custom-call(s32[8]{0:T(128)} %bitcast.27, s32[4,8]{1,0:T(4,128)} %bitcast.25, f32[4,8]{1,0:T(4,128)} %bitcast.26, ...), custom_call_target="tpu_custom_call" | custom-call | tf_op jit(solution)/shard_map/pallas_call | solution.py:519
  5.7 2.2 %collective-permute-done.other_ref = f32[8,4,256]{2,1,0:T(4,128)S(1)} collective-permute-done((f32[8,4,256]{2,1,0:T(4,128)}, f32[8,4,256]{2,1,0:T(4,128)S(1)}, u32[]{:S(2)}, u32[]{:S(2)}) %collective-permute-start) | collective-permute-done | bytes 32800 | tf_op jit(solution)/shard_map/ppermute | solution.py:36
  8.0 1.3 %shard_map.87 = (bf16[512,128]{1,0:T(8,128)(2,1)}, f32[32,512]{1,0:T(8,128)S(1)}) custom-call(f32[32,256]{1,0:T(8,128)S(1)} %get-tuple-element.25.own_ref, f32[8,4,256]{2,1,0:T(4,128)S(1)} %collective-permute-done.other_ref, f32[8,128]{1,0:T(8,128)S(1)} %get-tuple-element.26.table_ref, s32[8,128]{1,0:T(8,128)S(1)} %get-tuple-element.27.tile_rows_ref, ...), custom_call_target="tpu_custom_call" | custom-call | tf_op jit(solution)/shard_map/pallas_call | solution.py:519
  9.3 13.8 %all-to-all-start = ((bf16[128,4,128]{2,1,0:T(4,128)(2,1)}), bf16[128,4,128]{2,1,0:T(4,128)(2,1)S(1)}, u32[]{:S(2)}, u32[]{:S(2)}) async-start(bf16[128,4,128]{2,1,0:T(4,128)(2,1)} %bitcast.3), calls=%async_computation | async-start | bytes 262144 | tf_op jit(solution)/shard_map/all_to_all | solution.py:40
  23.8 3.1 %first_build.1 = (bf16[1536,1536]{1,0:T(8,128)(2,1)}, bf16[256,1536]{1,0:T(8,128)(2,1)}) custom-call(bf16[16,1536]{1,0:T(8,128)(2,1)S(1)} %get-tuple-element.30.left_ref, bf16[16,3072]{1,0:T(8,128)(2,1)S(1)} %get-tuple-element.31.right_ref), custom_call_target="tpu_custom_call" | custom-call | tf_op jit(solution)/shard_map/first_build/pallas_call | solution.py:541
  26.9 7.3 %all-to-all-done = bf16[128,4,128]{2,1,0:T(4,128)(2,1)S(1)} async-done(((bf16[128,4,128]{2,1,0:T(4,128)(2,1)}), bf16[128,4,128]{2,1,0:T(4,128)(2,1)S(1)}, u32[]{:S(2)}, u32[]{:S(2)}) %all-to-all-start) | async-done | bytes 131104 | tf_op jit(solution)/shard_map/all_to_all | solution.py:40
  34.2 1.6 %shard_map.88 = (bf16[512,128]{1,0:T(8,128)(2,1)}, bf16[256,512]{1,0:T(8,128)(2,1)S(1)}, s32[8,128]{1,0:T(8,128)S(1)}) custom-call(bf16[512,128]{1,0:T(8,128)(2,1)S(1)} %bitcast.18, f32[128,128]{1,0:T(8,128)S(1)} %copy-done.1, s32[1,8]{1,0:T(1,128)S(1)} %bitcast.24), custom_call_target="tpu_custom_call" | custom-call | tf_op jit(solution)/shard_map/pallas_call | solution.py:519
  35.8 6.3 %all-to-all-start.1 = ((bf16[128,4,128]{2,1,0:T(4,128)(2,1)}), bf16[128,4,128]{2,1,0:T(4,128)(2,1)S(1)}, u32[]{:S(2)}, u32[]{:S(2)}) async-start(bf16[128,4,128]{2,1,0:T(4,128)(2,1)} %bitcast.6), calls=%async_computation.1 | async-start | bytes 262144 | tf_op jit(solution)/shard_map/all_to_all | solution.py:40
  42.1 3.3 %second_build.1.refs_2_ = bf16[1280,1536]{1,0:T(8,128)(2,1)} custom-call(bf16[16,1536]{1,0:T(8,128)(2,1)S(1)} %get-tuple-element.30.left_ref, bf16[16,3072]{1,0:T(8,128)(2,1)S(1)} %get-tuple-element.31.right_ref), custom_call_target="tpu_custom_call" | custom-call | tf_op jit(solution)/shard_map/second_build/pallas_call | solution.py:558
  45.5 7.8 %all-to-all-done.1 = bf16[128,4,128]{2,1,0:T(4,128)(2,1)S(1)} async-done(((bf16[128,4,128]{2,1,0:T(4,128)(2,1)}), bf16[128,4,128]{2,1,0:T(4,128)(2,1)S(1)}, u32[]{:S(2)}, u32[]{:S(2)}) %all-to-all-start.1) | async-done | bytes 131104 | tf_op jit(solution)/shard_map/all_to_all | solution.py:40
  53.2 1.4 %copy-done.2 = bf16[8,512,256]{2,1,0:T(8,128)(2,1)} copy-done((bf16[8,512,256]{2,1,0:T(8,128)(2,1)}, bf16[8,512,256]{2,1,0:T(8,128)(2,1)S(1)}, u32[]{:S(2)}) %copy-start.2) | copy-done | bytes 2097176
  54.6 4.4 %shard_map.89 = (f32[32,512]{1,0:T(8,128)S(1)}, bf16[2,1536,1536]{2,1,0:T(8,128)(2,1)S(1)}, bf16[8,512,256]{2,1,0:T(8,128)(2,1)S(1)}) custom-call(bf16[512,128]{1,0:T(8,128)(2,1)S(1)} %bitcast.16, s32[8,128]{1,0:T(8,128)S(1)} %get-tuple-element.27.tile_rows_ref, s32[8,128]{1,0:T(8,128)S(1)} %get-tuple-element.36.other_rows_ref, ...), custom_call_target="tpu_custom_call" | custom-call | tf_op jit(solution)/shard_map/pallas_call | solution.py:519
  58.9 3.3 %collective-permute-start.3 = (f32[32,512]{1,0:T(8,128)S(1)}, f32[32,512]{1,0:T(8,128)S(1)}, u32[]{:S(2)}, u32[]{:S(2)}) collective-permute-start(f32[32,512]{1,0:T(8,128)S(1)} %get-tuple-element.39.mine_ref), channel_id=1, source_target_pairs={{0,1},{1,0},{2,3},{3,2},{4,5},{5,4},{6,7},{7,6},{8,9},{9,8},{10,11... | collective-permute-start | bytes 196616 | tf_op jit(solution)/shard_map/ppermute | solution.py:36
  62.3 0.9 collective-permute-done.3.theirs_ref
  63.2 1.9 %shard_map.90 = (bf16[512,128]{1,0:T(8,128)(2,1)S(1)}, f32[32,512]{1,0:T(8,128)S(1)}) custom-call(f32[32,512]{1,0:T(8,128)S(1)} %get-tuple-element.39.mine_ref, f32[32,512]{1,0:T(8,128)S(1)} %collective-permute-done.3.theirs_ref, bf16[8,512,256]{2,1,0:T(8,128)(2,1)S(1)} %copy-done, bf16[8,512,256]{2,1,0:T(8,128)(2,1)S(1)} %get-tuple-element.40.other_feet_ref, ...), custom_call_target="tpu_custom_call" | custom-call | tf_op jit(solution)/shard_map/pallas_call | solution.py:519
  65.0 17.1 %all_to_all.25 = bf16[128,4,128]{2,1,0:T(4,128)(2,1)S(1)} all-to-all(bf16[128,4,128]{2,1,0:T(4,128)(2,1)S(1)} %bitcast.22), channel_id=1, replica_groups=mesh['period'=128,'half'=2] {'period'}, dimensions={0} | all-to-all | bytes 262144 | tf_op jit(solution)/shard_map/all_to_all | solution.py:40
  82.9 16.8 %all_to_all.26 = bf16[128,4,128]{2,1,0:T(4,128)(2,1)S(1)} all-to-all(bf16[128,4,128]{2,1,0:T(4,128)(2,1)S(1)} %bitcast.20), channel_id=1, replica_groups=mesh['period'=128,'half'=2] {'period'}, dimensions={0} | all-to-all | bytes 262144 | tf_op jit(solution)/shard_map/all_to_all | solution.py:40
  99.6 1.8 %shard_map.92.mine_ref = f32[32,512]{1,0:T(8,128)S(1)} custom-call(bf16[512,128]{1,0:T(8,128)(2,1)S(1)} %bitcast.17, s32[8,128]{1,0:T(8,128)S(1)} %get-tuple-element.27.tile_rows_ref, s32[8,128]{1,0:T(8,128)S(1)} %get-tuple-element.36.other_rows_ref, bf16[2,1536,1536]{2,1,0:T(8,128)(2,1)S(1)} %get-tuple-element.43.refs_0_), custom_call_target="tpu_custom_call" | custom-call | tf_op jit(solution)/shard_map/pallas_call | solution.py:519
  101.4 3.0 %collective-permute-start.4 = (f32[32,512]{1,0:T(8,128)S(1)}, f32[32,512]{1,0:T(8,128)S(1)}, u32[]{:S(2)}, u32[]{:S(2)}) collective-permute-start(f32[32,512]{1,0:T(8,128)S(1)} %shard_map.92.mine_ref), channel_id=1, source_target_pairs={{0,1},{1,0},{2,3},{3,2},{4,5},{5,4},{6,7},{7,6},{8,9},{9,8},{10,11... | collective-permute-start | bytes 196616 | tf_op jit(solution)/shard_map/ppermute | solution.py:36
  104.4 0.9 collective-permute-done.4.theirs_ref
  105.3 1.5 %shard_map.93 = (f32[128,128]{1,0:T(8,128)S(1)}, f32[32,512]{1,0:T(8,128)S(1)}) custom-call(f32[32,512]{1,0:T(8,128)S(1)} %shard_map.92.mine_ref, f32[32,512]{1,0:T(8,128)S(1)} %collective-permute-done.4.theirs_ref, bf16[8,512,256]{2,1,0:T(8,128)(2,1)S(1)} %copy-done, bf16[8,512,256]{2,1,0:T(8,128)(2,1)S(1)} %get-tuple-element.40.other_feet_ref, ...), custom_call_target="tpu_custom_call" | custom-call | tf_op jit(solution)/shard_map/pallas_call | solution.py:519
  106.8 16.3 %all_to_all.27 = f32[128,1,128]{2,1,0:T(1,128)S(1)} all-to-all(f32[128,1,128]{2,1,0:T(1,128)S(1)} %bitcast.23), channel_id=1, replica_groups=mesh['period'=128,'half'=2] {'period'}, dimensions={0} | all-to-all | bytes 131072 | tf_op jit(solution)/shard_map/all_to_all | solution.py:40
  123.1 0.9 finish.1
  (12 shorter events, 1.6 us)
Async XLA Ops:
  0.6 52.6 %collective-permute-start.2 = (bf16[8,512,256]{2,1,0:T(8,128)(2,1)}, bf16[8,512,256]{2,1,0:T(8,128)(2,1)S(1)}, u32[]{:S(2)}, u32[]{:S(2)}) collective-permute-start(bf16[8,512,256]{2,1,0:T(8,128)(2,1)} %feet_ref.3), channel_id=1, source_target_pairs={{0,1},{1,0},{2,3},{3,2},{4,5},{5,4},{6,7},{7,6},{8,9},{9,8},{10,11... | collective-permute-start | bytes 6291464 | tf_op jit(solution)/shard_map/ppermute | solution.py:36
  3.9 4.0 %collective-permute-start = (f32[8,4,256]{2,1,0:T(4,128)}, f32[8,4,256]{2,1,0:T(4,128)S(1)}, u32[]{:S(2)}, u32[]{:S(2)}) collective-permute-start(f32[8,4,256]{2,1,0:T(4,128)} %own_in.1), channel_id=1, source_target_pairs={{0,1},{1,0},{2,3},{3,2},{4,5},{5,4},{6,7},{7,6},{8,9},{9,8},{10,11... | collective-permute-start | bytes 98312 | tf_op jit(solution)/shard_map/ppermute | solution.py:36
  4.0 19.0 %copy-start.3 = (s32[8,1]{0,1:T(1,128)S(1)}, s32[8,1]{0,1:T(1,128)}, u32[]{:S(2)}) copy-start(s32[8,1]{0,1:T(1,128)} %param.11) | copy-start | bytes 100
  4.0 30.2 %copy-start.1 = (f32[128,128]{1,0:T(8,128)S(1)}, f32[128,128]{1,0:T(8,128)}, u32[]{:S(2)}) copy-start(f32[128,128]{1,0:T(8,128)} %temporal_ref.3) | copy-start | bytes 196612
  9.3 25.0 %all-to-all-start = ((bf16[128,4,128]{2,1,0:T(4,128)(2,1)}), bf16[128,4,128]{2,1,0:T(4,128)(2,1)S(1)}, u32[]{:S(2)}, u32[]{:S(2)}) async-start(bf16[128,4,128]{2,1,0:T(4,128)(2,1)} %bitcast.3), calls=%async_computation | async-start | bytes 262144 | tf_op jit(solution)/shard_map/all_to_all | solution.py:40
  23.1 11.1 %collective-permute-start.1 = (s32[8]{0:T(128)S(1)}, s32[8]{0:T(128)S(1)}, u32[]{:S(2)}, u32[]{:S(2)}) collective-permute-start(s32[8]{0:T(128)S(1)} %bitcast.28), channel_id=1, source_target_pairs={{0,1},{1,0},{2,3},{3,2},{4,5},{5,4},{6,7},{7,6},{8,9},{9,8},{10,11... | collective-permute-start | bytes 104 | tf_op jit(solution)/shard_map/ppermute | solution.py:36
  35.8 17.4 %all-to-all-start.1 = ((bf16[128,4,128]{2,1,0:T(4,128)(2,1)}), bf16[128,4,128]{2,1,0:T(4,128)(2,1)S(1)}, u32[]{:S(2)}, u32[]{:S(2)}) async-start(bf16[128,4,128]{2,1,0:T(4,128)(2,1)} %bitcast.6), calls=%async_computation.1 | async-start | bytes 262144 | tf_op jit(solution)/shard_map/all_to_all | solution.py:40
  53.2 1.4 %copy-start.2 = (bf16[8,512,256]{2,1,0:T(8,128)(2,1)}, bf16[8,512,256]{2,1,0:T(8,128)(2,1)S(1)}, u32[]{:S(2)}) copy-start(bf16[8,512,256]{2,1,0:T(8,128)(2,1)S(1)} %collective-permute-done.2.refs_3_) | copy-start | bytes 6291460
  54.6 8.6 %copy-start = (bf16[8,512,256]{2,1,0:T(8,128)(2,1)S(1)}, bf16[8,512,256]{2,1,0:T(8,128)(2,1)}, u32[]{:S(2)}) copy-start(bf16[8,512,256]{2,1,0:T(8,128)(2,1)} %feet_ref.3) | copy-start | bytes 6291460
  58.9 4.2 %collective-permute-start.3 = (f32[32,512]{1,0:T(8,128)S(1)}, f32[32,512]{1,0:T(8,128)S(1)}, u32[]{:S(2)}, u32[]{:S(2)}) collective-permute-start(f32[32,512]{1,0:T(8,128)S(1)} %get-tuple-element.39.mine_ref), channel_id=1, source_target_pairs={{0,1},{1,0},{2,3},{3,2},{4,5},{5,4},{6,7},{7,6},{8,9},{9,8},{10,11... | collective-permute-start | bytes 196616 | tf_op jit(solution)/shard_map/ppermute | solution.py:36
  101.4 3.9 %collective-permute-start.4 = (f32[32,512]{1,0:T(8,128)S(1)}, f32[32,512]{1,0:T(8,128)S(1)}, u32[]{:S(2)}, u32[]{:S(2)}) collective-permute-start(f32[32,512]{1,0:T(8,128)S(1)} %shard_map.92.mine_ref), channel_id=1, source_target_pairs={{0,1},{1,0},{2,3},{3,2},{4,5},{5,4},{6,7},{7,6},{8,9},{9,8},{10,11... | collective-permute-start | bytes 196616 | tf_op jit(solution)/shard_map/ppermute | solution.py:36
